TPU v7x, 32 devices: a whole 2x2x4 slice. The times are simulated.
32 devices in a mesh: dp: 8 (over y, x, core), tp: 4 (over z).
Axes of the slice: x: 2, y: 2, z: 4, core: 2. Of those that a mesh axis runs over, the one named last changes fastest.
Arguments:
- tokens: bfloat16 [8, 512, 768], P('dp', 'tp'), may hold values from -6 to 6
- seg_ids: int32 [8, 512], P('dp'), may hold values from 0 to 2, never falling along the last dimension, each value on 1 to 256 neighbouring positions
- time_embed: float32 [8, 3, 768], P('dp'), may hold values from -6 to 6
- text_states: bfloat16 [8, 3, 64, 768], P('dp', None, 'tp'), may hold values from -6 to 6
- text_lengths: int32 [8, 3], P('dp'), may hold values from 16 to 64, as said below
- out_grad: bfloat16 [8, 512, 768], P('dp', 'tp'), may hold values from -6 to 6
- w_qkv: bfloat16 [768, 2304], P(None, 'tp'), may hold values from -0.21875 to 0.21875
- w_attn_out: bfloat16 [768, 768], P('tp'), may hold values from -3 to 3
- b_attn_out: bfloat16 [768], replicated, may hold values from -3 to 3
- w_cross_q: bfloat16 [768, 768], P(None, 'tp'), may hold values from -0.21875 to 0.21875
- w_cross_kv: bfloat16 [768, 1536], P(None, 'tp'), may hold values from -0.21875 to 0.21875
- w_cross_out: bfloat16 [768, 768], P('tp'), may hold values from -0.875 to 0.875
- b_cross_out: bfloat16 [768], replicated, may hold values from -3 to 3
- w_up: bfloat16 [768, 3072], P(None, 'tp'), may hold values from -0.21875 to 0.21875
- b_up: bfloat16 [3072], P('tp'), may hold values from -3 to 3
- w_down: bfloat16 [3072, 768], P('tp'), may hold values from -0.109375 to 0.109375
- w_mod: bfloat16 [768, 4608], P(None, 'tp'), may hold values from -0.21875 to 0.21875
- b_mod: bfloat16 [4608], P('tp'), may hold values from -3 to 3
Outputs:
- d_tokens: bfloat16 [8, 512, 768], P('dp', 'tp')
- d_time: float32 [8, 3, 768], P('dp')
- d_text: bfloat16 [8, 3, 64, 768], P('dp', None, 'tp')
- g_qkv: float32 [768, 2304], P(None, 'tp')
- g_attn_out: float32 [768, 768], P('tp')
- gb_attn_out: float32 [768], replicated
- g_cross_q: float32 [768, 768], P(None, 'tp')
- g_cross_kv: float32 [768, 1536], P(None, 'tp')
- g_cross_out: float32 [768, 768], P('tp')
- gb_cross_out: float32 [768], replicated
- g_up: float32 [768, 3072], P(None, 'tp')
- gb_up: float32 [3072], P('tp')
- g_down: float32 [3072, 768], P('tp')
- g_mod: float32 [768, 4608], P(None, 'tp')
- gb_mod: float32 [4608], P('tp')
Inputs may be any that keep to these rules, and one draw needn't show every extreme that they name: `seg_ids`: along a group's row item numbers never fall and every item of 0 to 2 has 1 to 256 frames. `text_lengths`: in every group one item has all 64 text tokens valid.
All inputs are finite; a program needn't handle non-finite values.
Results may differ from a plain program's by a relative error of at most 0.02.
Values may be sent and summed in bfloat16 or wider, within the bound.
A program may use at most 128 MiB of HBM per device.

v0:
```python
import functools
import math

import jax
import jax.numpy as jnp
from jax import lax
from jax.experimental import pallas as pl
from jax.experimental.pallas import tpu as pltpu
from jax.sharding import PartitionSpec as P

DH = 64
TP = 4
MESH = pl.DeviceIdType.MESH
BF = jnp.bfloat16
F32 = jnp.float32
GELU_C = math.sqrt(2.0 / math.pi)


def dot_nn(left, right):
    return jnp.dot(left, right, preferred_element_type=F32)


def dot_tn(left, right):
    return lax.dot_general(left, right, (((0,), (0,)), ((), ())), preferred_element_type=F32)


def dot_nt(left, right):
    return lax.dot_general(left, right, (((1,), (1,)), ((), ())), preferred_element_type=F32)


def normalize(values):
    center = values - jnp.mean(values, axis=-1, keepdims=True)
    inverse = lax.rsqrt(jnp.mean(center * center, axis=-1, keepdims=True) + 1e-06)
    return center * inverse, inverse


def normalize_back(grad, normed, inverse):
    return inverse * (
        grad
        - jnp.mean(grad, axis=-1, keepdims=True)
        - normed * jnp.mean(grad * normed, axis=-1, keepdims=True)
    )


def bucket_rows(hidden, heads_width):
    sizes = [
        ("up", hidden),
        ("down", hidden),
        ("cross_out", heads_width),
        ("cross_q", heads_width),
        ("cross_kv", 2 * heads_width),
        ("attn_out", heads_width),
        ("qkv", 3 * heads_width),
    ]
    at, place = 0, {}
    for name, rows in sizes:
        place[name] = (at, rows)
        at += rows
    return place, at


def layer_kernel(
    dims,
    tok_h, og_h, text_h, wqkvT_h, wo_h, wcqT_h, wckv_h, wco_h, wup_h, wdn_h, wmod_h,
    seg_ref, time_ref, b_attn_out_ref, b_cross_out_ref, b_up_ref, b_mod_ref, tlen_ref,
    dtok_o, dtime_o, dtext_o, grads_o, early_o, late_o,
    tok, og, text, att, gc,
    wqkvT, wckv, wfull, wup, wdn, wmod,
    modbuf, mods, segrow, segcol, onehot, ktag,
    attn_in, na, qkvT, kvx, pself,
    stream_a, inv_c, cross_in, cqT, ckvT, kx, vx, pcross, catT, branch_own,
    mlp_in, nm_own, invm_own, act, dpre, dbm, rs_send, rs_recv,
    gc_own, dcT, dcqT, dckv, dckvT, grad_own, dba, dOT, dqkvT, dkv_acc,
    rs2_send, rs2_recv, dm, dmp, dmr, dsil, dsr, early, eall, lall,
    grads, rbuf,
    lsem, ssem, rsem, csem_s, csem_r, wsem_s, wsem_r, gsem_s, gsem_r, esem_s, esem_r, osem,
):
    dp_count, place, items = dims
    tp = lax.axis_index("tp")
    dp = lax.axis_index("dp")
    R = tok.shape[1]
    D = tok.shape[2]
    T = TP * R
    HW = att.shape[1]
    HL = HW // DH
    TK = TP * text.shape[1]
    TL = text.shape[1]
    HEADS = TP * HL
    MB = modbuf.shape[2]
    QB = 2 * R
    scale = 1.0 / math.sqrt(DH)
    sub = lax.rem(dp, 8)
    base8 = dp - sub
    core = lax.rem(sub, 2)
    chip = sub // 2

    def tp_peer(k):
        return {"tp": lax.rem(tp + k, TP)}

    def remote(src, dst, send, recv, peer):
        return pltpu.make_async_remote_copy(
            src_ref=src, dst_ref=dst, send_sem=send, recv_sem=recv, device_id=peer, device_id_type=MESH
        )

    def span(at, size, unit):
        return pl.ds(pl.multiple_of(at, unit), size)

    loads = [
        (tok_h, tok.at[0]),
        (wmod_h, wmod),
        (text_h, text.at[0]),
        (wqkvT_h, wqkvT),
        (wcqT_h, wfull.at[0, 1]),
        (wo_h, wfull.at[0, 0]),
        (wco_h, wfull.at[0, 2]),
        (wckv_h, wckv),
        (og_h, og.at[0]),
        (wup_h, wup),
        (wdn_h, wdn),
    ]
    local = [pltpu.make_async_copy(src, dst, lsem.at[i]) for i, (src, dst) in enumerate(loads)]
    for copy in local:
        copy.start()

    barrier = pltpu.get_barrier_semaphore()
    for k in range(1, TP):
        pl.semaphore_signal(barrier, inc=1, device_id=tp_peer(k), device_id_type=MESH)

    def greet(k, carry):
        pl.semaphore_signal(
            barrier, inc=1, device_id={"dp": lax.rem(dp + k, dp_count)}, device_id_type=MESH
        )
        return carry

    lax.fori_loop(1, dp_count, greet, 0)

    early[...] = jnp.zeros(early.shape, F32)
    for item in range(items):
        early[item : item + 1, :] = time_ref[item]
    time = early[...]
    sig = 1.0 / (1.0 + jnp.exp(-time))
    silu_low = (time * sig).astype(BF)
    early[...] = silu_low.astype(F32)
    local[1].wait()
    modbuf[tp] = dot_nn(silu_low, wmod[...]) + b_mod_ref[...].astype(F32).reshape(1, MB)
    local[0].wait()

    pl.semaphore_wait(barrier, TP - 1 + dp_count - 1)

    pending, chains = [], []
    inner = (tp > 0) & (tp < TP - 1)
    slot_a = jnp.where(tp == 3, 3, 1)
    slot_b = jnp.where((tp == 0) | (tp == 3), 2, 3)
    slot_c = jnp.where(tp == 0, 3, jnp.where(tp == 3, 1, 2))
    right, left = {"tp": lax.rem(tp + 1, TP)}, {"tp": lax.rem(tp + TP - 1, TP)}
    onward = {"tp": jnp.where(tp == 1, 0, TP - 1)}
    onward_slot = jnp.where(tp == 1, 3, 1)

    class Chain:
        def __init__(self, index, view):
            self.index, self.view, self.started = index, view, []
            chains.append(self)

        def copy(self, src, dst, send, chunk, peer):
            return remote(
                self.view(src, chunk), self.view(dst, chunk),
                csem_s.at[self.index, send, chunk], csem_r.at[self.index, dst, chunk], peer,
            )

        def start(self, chunk):
            self.started.append(chunk)

            @pl.when(tp < TP - 1)
            def _():
                self.copy(0, 3, 0, chunk, right).start()

            @pl.when(tp > 0)
            def _():
                self.copy(0, 1, 1, chunk, left).start()

        def step(self, which, chunk):
            slot = (slot_a, slot_b, slot_c)[which]
            self.copy(slot, slot, 2 + which, chunk, right).wait_recv()

            @pl.when(inner)
            def _():
                if which == 0:
                    self.copy(slot, 2, 2, chunk, left).start()
                elif which == 1:
                    self.copy(slot, 2, 3, chunk, right).start()
                else:
                    self.copy(slot, onward_slot, 4, chunk, onward).start()

        def finish(self):
            for chunk in self.started:

                @pl.when(tp < TP - 1)
                def _():
                    self.copy(0, 3, 0, chunk, right).wait_send()

                @pl.when(tp > 0)
                def _():
                    self.copy(0, 1, 1, chunk, left).wait_send()

                @pl.when(inner)
                def _():
                    self.copy(slot_a, 2, 2, chunk, left).wait_send()
                    self.copy(slot_b, 2, 3, chunk, right).wait_send()
                    self.copy(slot_c, onward_slot, 4, chunk, onward).wait_send()

    half = R // 2
    tok_chain = Chain(0, lambda slot, c: tok.at[slot, c * half : (c + 1) * half])
    text_chain = Chain(1, lambda slot, c: text.at[slot])
    WR, WC = HW // 4, D // 2
    wrow = pl.multiple_of(chip * WR, 16)
    wcol = pl.multiple_of(core * WC, 128)
    pieces = (slice(0, 3), slice(3, 5))
    w_chain = Chain(2, lambda slot, c: wfull.at[slot, pieces[c], pl.ds(wrow, WR), pl.ds(wcol, WC)])
    att_chain = Chain(3, lambda slot, c: att.at[slot, c * DH : (c + 1) * DH])
    og_chain = Chain(4, lambda slot, c: og.at[slot, c * half : (c + 1) * half])
    gc_chain = Chain(5, lambda slot, c: gc.at[slot, c * half : (c + 1) * half])

    def direct(tag, src_of, dst_of):
        copies = []
        for k in range(1, TP):
            copy = remote(src_of(k), dst_of(k), ssem.at[tag, k], rsem.at[tag, TP - k], tp_peer(k))
            copy.start()
            copies.append(copy)
        pending.extend(copies)
        return copies

    def arrived(copies, slot):
        copies[TP - 1 - slot].wait_recv()

    tok_chain.start(0)
    tok_chain.start(1)
    mod_copies = direct(0, lambda k: modbuf.at[tp], lambda k: modbuf.at[tp])

    eye = lax.broadcasted_iota(jnp.int32, (R, R), 0) == lax.broadcasted_iota(jnp.int32, (R, R), 1)
    for slot in range(TP):
        owner = lax.rem(tp + slot, TP)
        row = seg_ref[:, pl.ds(pl.multiple_of(owner * R, R), R)].astype(F32)
        segrow[:, slot * R : (slot + 1) * R] = row
        col = jnp.sum(jnp.where(eye, row, 0.0), axis=1, keepdims=True)
        segcol[slot * R : (slot + 1) * R, :] = col
    kinds = lax.broadcasted_iota(jnp.int32, (16, T), 0)
    matches = (segrow[...] == kinds.astype(F32)) & (kinds < items)
    onehot[...] = jnp.where(matches | (kinds == items), 1.0, 0.0).astype(BF)
    key_at = lax.broadcasted_iota(jnp.int32, (TK, 1), 0)
    key_slot = key_at // TL
    key_item = lax.rem(key_at, TL) // (TL // items)
    key_pos = lax.rem(key_slot + tp, TP) * (TL // items) + lax.rem(key_at, TL // items)
    tag = jnp.full((TK, 1), -1.0, F32)
    for item in range(items):
        inside = (key_item == item) & (key_pos < tlen_ref[0, item])
        tag = jnp.where(inside, float(item), tag)
    ktag[...] = tag

    for k in range(1, TP):
        arrived(mod_copies, k)
    for j in range(6):
        lo, hi = j * D, (j + 1) * D
        at = lo
        while at < hi:
            block = at // MB
            end = min(hi, (block + 1) * MB)
            mods[j, :, at - lo : end - lo] = modbuf[block, :, at - block * MB : end - block * MB]
            at = end

    def per_frame(j, rows):
        col = segcol[rows, :]
        out = mods[j, items - 1 : items, :]
        for item in range(items - 2, -1, -1):
            out = jnp.where(col == float(item), mods[j, item : item + 1, :], out)
        return out

    def item_sums(rows, values):
        return dot_nn(onehot[:, rows], values.astype(BF))

    own = slice(0, R)
    local[3].wait()

    def project(slot):
        rows = span(slot * R, R, R)
        normed, inverse = normalize(tok[slot].astype(F32))
        na[rows, :] = normed.astype(BF)
        x = (normed * (1.0 + per_frame(1, rows)) + per_frame(0, rows)).astype(BF)
        attn_in[rows, :] = x
        qkvT[:, rows] = dot_nt(wqkvT[...], x).astype(BF)

    project(0)
    for which, slot in enumerate((slot_a, slot_b, slot_c)):
        tok_chain.step(which, 0)
        tok_chain.step(which, 1)
        if which == 0:
            local[2].wait()
            local[7].wait()
            ident = (
                lax.broadcasted_iota(jnp.int32, (D, D), 0) == lax.broadcasted_iota(jnp.int32, (D, D), 1)
            ).astype(F32).astype(BF)
            wckvT = dot_tn(wckv[...], ident).astype(BF)
            wfull[0, 3] = wckvT[:HW]
            wfull[0, 4] = wckvT[HW:]
            for copy in local[4:7]:
                copy.wait()
        if which == 2:
            text_chain.start(0)
            w_chain.start(0)
            w_chain.start(1)
        project(slot)

    for h in range(HL):
        q0 = h * 3 * DH
        keys = (qkvT[q0 + DH : q0 + 2 * DH, :].astype(F32).T * scale).astype(BF)
        kvx[2 * h] = keys
        kvx[2 * h + 1] = qkvT[q0 + 2 * DH : q0 + 3 * DH, :].astype(F32).T.astype(BF)

        def attend(b, carry, h=h, q0=q0):
            cols = span(b * R, R, R)
            scores = dot_nn(kvx[2 * h], qkvT[q0 : q0 + DH, cols])
            scores = jnp.where(segcol[...] == segrow[:, cols], scores, -1000000000.0)
            peak = jnp.max(scores, axis=0, keepdims=True)
            exponent = jnp.exp(scores - peak)
            probs = exponent * (1.0 / jnp.sum(exponent, axis=0, keepdims=True))
            pself[h, :, cols] = probs
            att[0, h * DH : (h + 1) * DH, cols] = dot_nn(
                qkvT[q0 + 2 * DH : q0 + 3 * DH, :], probs.astype(BF)
            ).astype(BF)
            return carry

        lax.fori_loop(0, TP, attend, 0)
        att_chain.start(h)
        if h == 0:
            text_chain.step(0, 0)
        if h == 1:
            w_chain.step(0, 0)
            text_chain.step(1, 0)
        if h == 2:
            w_chain.step(0, 1)
    w_chain.step(1, 0)
    w_chain.step(1, 1)
    text_chain.step(2, 0)
    for h in range(HL):
        att_chain.step(0, h)
    w_chain.step(2, 0)
    w_chain.step(2, 1)
    local[8].wait()

    wx = []
    for m in range(1, 4):
        peer = {"dp": base8 + jnp.bitwise_xor(sub, 2 * m)}
        copy = remote(
            wfull.at[1:TP, :, pl.ds(wrow, WR), pl.ds(wcol, WC)],
            wfull.at[1:TP, :, pl.ds(wrow, WR), pl.ds(wcol, WC)],
            wsem_s.at[m], wsem_r.at[m], peer,
        )
        copy.start()
        wx.append(copy)
    for h in range(HL):
        att_chain.step(1, h)
    og_chain.start(0)
    og_chain.start(1)
    for copy in wx:
        copy.wait_recv()
    wlast = remote(
        wfull.at[1:TP, :, :, pl.ds(wcol, WC)],
        wfull.at[1:TP, :, :, pl.ds(wcol, WC)],
        wsem_s.at[0], wsem_r.at[0], {"dp": base8 + jnp.bitwise_xor(sub, 1)},
    )
    wlast.start()
    pending.extend(wx + [wlast])
    wlast.wait_recv()

    def full(i):
        return wfull[:, i].reshape(TP * HW, D)

    text_flat = text[...].reshape(TK, D)
    for s in range(TP):
        for part in range(2):
            ckvT[(2 * s + part) * HW : (2 * s + part + 1) * HW, :] = dot_nt(wfull[s, 3 + part], text_flat).astype(BF)
    for h in range(HEADS):
        pair = ckvT[h * 2 * DH : (h + 1) * 2 * DH, :].astype(F32).T
        kx[h] = (pair[:, :DH] * scale).astype(BF)
        vx[h] = pair[:, DH:].astype(BF)
    for h in range(HL):
        att_chain.step(2, h)

    b_attn_out = b_attn_out_ref[...].astype(F32).reshape(1, D)
    b_cross_out = b_cross_out_ref[...].astype(F32).reshape(1, D)
    b_up = b_up_ref[...].astype(F32).reshape(1, wup.shape[1])

    def forward(i, carry):
        rows = span(i * QB, QB, QB)
        parts = []
        for b in range(QB // R):
            at = i * (QB // R) + b
            parts.append(
                jnp.concatenate(
                    [att[k, :, span(lax.rem(at + TP - k, TP) * R, R, R)] for k in range(TP)], axis=0
                )
            )
        branch = dot_tn(jnp.concatenate(parts, axis=1), full(0)) + b_attn_out

        @pl.when(i == 0)
        def _():
            branch_own[...] = branch[:R]

        frames = tok[span(i * (QB // R), QB // R, 1)].reshape(QB, D)
        stream_a[rows, :] = frames.astype(F32) + per_frame(2, rows) * branch
        normed, inverse = normalize(stream_a[rows, :])
        inv_c[rows, :] = inverse
        x = normed.astype(BF)
        cross_in[rows, :] = x
        cqT[:, rows] = dot_nt(full(1), x).astype(BF)
        allowed = ktag[...] == segrow[:, rows]
        for h in range(HEADS):
            hr = slice(h * DH, (h + 1) * DH)
            scores = dot_nn(kx[h], cqT[hr, rows])
            scores = jnp.where(allowed, scores, -1000000000.0)
            peak = jnp.max(scores, axis=0, keepdims=True)
            exponent = jnp.exp(scores - peak)
            probs = exponent * (1.0 / jnp.sum(exponent, axis=0, keepdims=True))
            pcross[h, :, rows] = probs
            vT = ckvT[h * 2 * DH + DH : (h + 1) * 2 * DH, :]
            catT[hr, rows] = dot_nn(vT, probs.astype(BF)).astype(BF)
        stream = stream_a[rows, :] + dot_tn(catT[:, rows], full(2)) + b_cross_out
        normed, inverse = normalize(stream)

        @pl.when(i == 0)
        def _():
            nm_own[...] = normed[:R]
            invm_own[...] = inverse[:R]

        mlp_in[rows, :] = (normed * (1.0 + per_frame(4, rows)) + per_frame(3, rows)).astype(BF)
        for which in range(2):

            @pl.when(i == which)
            def _():
                og_chain.step(which, 0)
                og_chain.step(which, 1)

        return carry

    lax.fori_loop(0, T // QB, forward, 0)
    og_chain.step(2, 0)
    og_chain.step(2, 1)

    local[9].wait()
    local[10].wait()
    dm[5] = jnp.zeros((16, D), F32)

    def rs_copy(b):
        return remote(
            rs_send.at[b], rs_recv.at[TP - 1 - b], ssem.at[1, b], rsem.at[1, TP - b], tp_peer(b)
        )

    def feed(i, carry):
        b = jnp.where(i == 0, 2, jnp.where(i == 3, 0, 2 * i - 1))
        rows = span(b * R, R, R)
        pre = dot_nn(mlp_in[rows, :], wup[...]) + b_up
        square = pre * pre
        bend = jnp.tanh(GELU_C * pre * (1.0 + 0.044715 * square))
        low = (0.5 * pre * (1.0 + bend)).astype(BF)
        act[rows, :] = low
        slope = 0.5 * (1.0 + bend) + 0.5 * pre * (1.0 - bend * bend) * (
            GELU_C * (1.0 + 3.0 * 0.044715 * square)
        )
        grad = og[b].astype(F32)
        d_branch = (grad * per_frame(5, rows)).astype(BF)
        dbm[rows, :] = d_branch
        d_pre = (dot_nt(d_branch, wdn[...]) * slope).astype(BF)
        dpre[rows, :] = d_pre
        rs_send[b] = dot_nt(d_pre, wup[...]).astype(BF)

        @pl.when(i < 3)
        def _():
            rs_copy(b).start()

        dm[5] += item_sums(rows, grad * dot_nn(low, wdn[...]))
        return carry

    lax.fori_loop(0, TP, feed, 0)
    rs_copies = {b: rs_copy(b) for b in range(1, TP)}
    pending.extend(rs_copies.values())
    early[3:4, :] = dot_nn(onehot[...], dpre[...])[items : items + 1, :]

    bits = []
    step = 8
    while step < dp_count:
        bits.append(step)
        step *= 2

    class Reduce:
        def __init__(self, index, start, rows, room):
            self.parts = []
            half = rows // 2
            for part in range(2):
                chain = (1, 2, 4) if part == 0 else (1, 4, 2)
                self.parts.append((start + part * half, half, chain, part * half))
            self.index, self.room = index, room
            self.open, self.own = [], []

        def sem(self, part, step):
            return gsem_s.at[self.index, part, step], gsem_r.at[self.index, part, step]

        def launch(self, src, dst, part, step, bit):
            send, recv = self.sem(part, step)
            copy = remote(src, dst, send, recv, {"dp": jnp.bitwise_xor(dp, bit)})
            copy.start()
            pending.append(copy)
            return copy

        def bounds(self, part, level):
            start, rows, chain, _ = self.parts[part]
            at, size = start, rows
            for bit in chain[:level]:
                size //= 2
                at = at + jnp.bitwise_and(dp // bit, 1) * size
            return at, size

        def scatter_start(self, level):
            self.open = []
            for part in range(2):
                at, size = self.bounds(part, level)
                bit = self.parts[part][2][level]
                half = size // 2
                mine = jnp.bitwise_and(dp // bit, 1)
                other = pl.multiple_of(at + (1 - mine) * half, 16)
                rows = self.parts[part][1]
                room = self.room + 2 * (rows - (rows >> level)) + part * half
                copy = self.launch(
                    grads.at[pl.ds(other, half)], rbuf.at[room : room + half], part, level, bit
                )
                self.open.append((copy, room, half))

        def scatter_end(self, level):
            for part in range(2):
                copy, room, half = self.open[part]
                copy.wait_recv()
                at, size = self.bounds(part, level + 1)
                mine = pl.ds(pl.multiple_of(at, 16), half)
                grads[mine, :] = (grads[mine, :].astype(F32) + rbuf[room : room + half, :].astype(F32)).astype(BF)

        def widen(self):
            for i, bit in enumerate(bits):
                for part in range(2):
                    at, size = self.bounds(part, 3)
                    rows = self.parts[part][1]
                    mine = pl.ds(pl.multiple_of(at, 16), size)
                    room = self.room + 2 * (rows - rows // 8) + (2 * i + part) * size
                    copy = self.launch(grads.at[mine], rbuf.at[room : room + size], part, 6 + i, bit)
                    copy.wait_recv()
                    grads[mine, :] = (
                        grads[mine, :].astype(F32) + rbuf[room : room + size, :].astype(F32)
                    ).astype(BF)

        def gather_start(self, level):
            self.open = []
            source = grads if level == 2 else grads_o
            if level == 1:
                for copy in self.own:
                    copy.wait()
            for part in range(2):
                at, size = self.bounds(part, level + 1)
                bit = self.parts[part][2][level]
                mine = pl.ds(pl.multiple_of(at, 16), size)
                self.open.append(
                    self.launch(source.at[mine], grads_o.at[mine], part, 3 + (2 - level), bit)
                )
                if level == 2:
                    copy = pltpu.make_async_copy(grads.at[mine], grads_o.at[mine], osem.at[self.index, part])
                    copy.start()
                    self.own.append(copy)

        def gather_end(self):
            for copy in self.open:
                copy.wait_recv()

    mid0 = place["cross_out"][0]
    mid1 = place["attn_out"][0]
    total_rows = grads.shape[0]
    extra = 2 * len(bits)
    rooms, at = [], 0
    for rows in (mid0, mid1 - mid0, total_rows - mid1):
        rooms.append(at)
        at += rows - rows // 8 + extra * (rows // 16)
    reduce_mlp = Reduce(0, 0, mid0, rooms[0])
    reduce_cross = Reduce(1, mid0, mid1 - mid0, rooms[1])
    reduce_self = Reduce(2, mid1, total_rows - mid1, rooms[2])

    def put(name, values):
        at, rows = place[name]
        grads[at : at + rows, :] = values.astype(BF)

    put("up", dot_tn(mlp_in[...], dpre[...]))
    put("down", dot_tn(act[...], dbm[...]))
    reduce_mlp.scatter_start(0)

    d_mlp = rs_send[0].astype(F32)
    reduce_mlp.scatter_end(0)
    reduce_mlp.scatter_start(1)
    for k in (1, 3, 2):
        rs_copies[TP - k].wait_recv()
        d_mlp = d_mlp + rs_recv[k - 1].astype(F32)
    normed = nm_own[...]
    grad_c = og[0].astype(F32) + normalize_back(d_mlp * (1.0 + per_frame(4, own)), normed, invm_own[...])
    gc_own[...] = grad_c
    gc[0] = grad_c.astype(BF)
    gc_chain.start(0)
    gc_chain.start(1)
    dm[3] = item_sums(own, d_mlp)
    dm[4] = item_sums(own, d_mlp * normed)

    dckv[...] = jnp.zeros(dckv.shape, F32)
    GROUP = 4

    def backward(slot, first):
        rows = span(slot * R, R, R)
        grad_low = gc[slot]
        dcT[:, rows] = dot_nt(full(2), grad_low).astype(BF)

        def heads(g, carry):
            for j in range(GROUP):
                h = g * GROUP + j
                hr = span(h * DH, DH, DH)
                kr, vr = span(h * 2 * DH, DH, DH), span(h * 2 * DH + DH, DH, DH)
                d_out = dcT[hr, rows]
                probs = pcross[h, :, rows]
                d_probs = dot_nn(vx[h], d_out)
                d_scores = (probs * (d_probs - jnp.sum(probs * d_probs, axis=0, keepdims=True))).astype(BF)
                dcqT[hr, rows] = (dot_nn(ckvT[kr, :], d_scores) * scale).astype(BF)
                dckv[kr, :] += dot_nt(cqT[hr, rows], d_scores) * scale
                dckv[vr, :] += dot_nt(d_out, probs.astype(BF))
            return carry

        lax.fori_loop(0, HEADS // GROUP, heads, 0)
        d_cross = dot_tn(dcqT[:, rows], full(1))
        grad = gc_own[...] if first else grad_low.astype(F32)
        grad = grad + normalize_back(d_cross, cross_in[rows, :].astype(F32), inv_c[rows, :])
        if first:
            grad_own[...] = grad
            dm[2] = item_sums(own, grad * branch_own[...])
        low = (grad * per_frame(2, rows)).astype(BF)
        dba[rows, :] = low
        dOT[:, rows] = dot_nt(wfull[0, 0], low).astype(BF)

    backward(0, True)
    gc_chain.step(0, 0)
    gc_chain.step(0, 1)
    gc_chain.step(1, 0)
    gc_chain.step(1, 1)
    reduce_mlp.scatter_end(1)
    reduce_mlp.scatter_start(2)
    backward(slot_a, False)
    gc_chain.step(2, 0)
    gc_chain.step(2, 1)
    reduce_mlp.scatter_end(2)
    reduce_mlp.widen()
    reduce_mlp.gather_start(2)
    backward(slot_b, False)
    reduce_mlp.gather_end()
    reduce_mlp.gather_start(1)
    backward(slot_c, False)

    gc_flat = gc[...].reshape(T, D)
    dckvT[...] = dckv[...].astype(BF)
    put("cross_out", dot_nn(catT[0:HW, :], gc_flat))
    put("cross_q", dot_nn(dcqT[0:HW, :], cross_in[...]))
    put("cross_kv", dot_nn(dckvT[0 : 2 * HW, :], text_flat))
    put("attn_out", dot_nn(att[0], dba[...]))
    reduce_cross.scatter_start(0)
    early[4:5, :] = dot_nn(onehot[...], gc_flat)[items : items + 1, :]
    early[5:6, :] = dot_nn(onehot[...], dba[...])[items : items + 1, :]
    eall[dp] = early[...]

    def dp_send(src, dst, index):
        def one(k, carry):
            peer = lax.rem(dp + k, dp_count)
            remote(
                src, dst, esem_s.at[index, k], esem_r.at[index, dp_count - k], {"dp": peer}
            ).start()
            return carry

        lax.fori_loop(1, dp_count, one, 0)

    def dp_wait(src, dst, index):
        def one(k, carry):
            remote(
                src, dst, esem_s.at[index, k], esem_r.at[index, k], {"dp": lax.rem(dp + k, dp_count)}
            ).wait()
            return carry

        lax.fori_loop(1, dp_count, one, 0)

    dp_send(eall.at[dp], eall.at[dp], 0)

    for h in range(HL):
        q0 = h * 3 * DH
        hr = slice(h * DH, (h + 1) * DH)
        dkv_acc[...] = jnp.zeros(dkv_acc.shape, F32)

        def attend_back(b, carry, h=h, q0=q0, hr=hr):
            cols = span(b * R, R, R)
            d_out = dOT[hr, cols]
            probs = pself[h, :, cols]
            d_probs = dot_nn(kvx[2 * h + 1], d_out)
            d_scores = (probs * (d_probs - jnp.sum(probs * d_probs, axis=0, keepdims=True))).astype(BF)
            dqkvT[q0 : q0 + DH, cols] = (dot_nn(qkvT[q0 + DH : q0 + 2 * DH, :], d_scores) * scale).astype(BF)
            dkv_acc[0:DH, :] += dot_nt(qkvT[q0 : q0 + DH, cols], d_scores) * scale
            dkv_acc[DH : 2 * DH, :] += dot_nt(d_out, probs.astype(BF))
            return carry

        lax.fori_loop(0, TP, attend_back, 0)
        dqkvT[q0 + DH : q0 + 3 * DH, :] = dkv_acc[...].astype(BF)
        if h == 0:
            reduce_cross.scatter_end(0)
            reduce_cross.scatter_start(1)
            reduce_mlp.gather_end()
            reduce_mlp.gather_start(0)

    dm[0] = jnp.zeros((16, D), F32)
    dm[1] = jnp.zeros((16, D), F32)

    def rs2_copy(b):
        return remote(
            rs2_send.at[b], rs2_recv.at[TP - 1 - b], ssem.at[2, b], rsem.at[2, TP - b], tp_peer(b)
        )

    def entry(i, carry):
        b = jnp.where(i == 0, 2, jnp.where(i == 3, 0, 2 * i - 1))
        rows = span(b * R, R, R)
        part = dot_tn(dqkvT[:, rows], wqkvT[...])
        rs2_send[b] = part.astype(BF)

        @pl.when(i < 3)
        def _():
            rs2_copy(b).start()

        dm[0] += item_sums(rows, part)
        dm[1] += item_sums(rows, part * na[rows, :].astype(F32))
        return carry

    lax.fori_loop(0, TP, entry, 0)
    rs2_copies = {b: rs2_copy(b) for b in range(1, TP)}
    pending.extend(rs2_copies.values())

    put("qkv", dot_nn(dqkvT[...], attn_in[...]))
    reduce_self.scatter_start(0)

    for j in range(6):
        lo, hi = j * D, (j + 1) * D
        at = lo
        while at < hi:
            block = at // MB
            end = min(hi, (block + 1) * MB)
            dmp[block, :, at - block * MB : end - block * MB] = dm[j, 0:8, at - lo : end - lo]
            at = end
    dm_copies = direct(
        3, lambda k: dmp.at[lax.rem(tp + k, TP)], lambda k: dmr.at[TP - 1 - k]
    )
    reduce_self.scatter_end(0)
    reduce_self.scatter_start(1)
    reduce_cross.scatter_end(1)
    reduce_cross.scatter_start(2)

    dtext_o[...] = dot_tn(dckvT[:, 0:TL], wfull[:, 3:5].reshape(TP * 2 * HW, D)).astype(BF)

    d_mod = dmp[tp]
    for k in range(1, TP):
        arrived(dm_copies, k)
        d_mod = d_mod + dmr[k - 1]
    low = d_mod.astype(BF)
    lall[dp] = low.astype(F32)
    dp_send(lall.at[dp], lall.at[dp], 1)
    dsil[...] = dot_nt(low, wmod[...])
    ds_copies = direct(4, lambda k: dsil, lambda k: dsr.at[TP - 1 - k])

    reduce_self.scatter_end(1)
    reduce_self.scatter_start(2)
    reduce_cross.scatter_end(2)
    reduce_cross.widen()
    reduce_cross.gather_start(2)
    reduce_mlp.gather_end()
    reduce_self.scatter_end(2)
    reduce_self.widen()
    reduce_self.gather_start(2)
    reduce_cross.gather_end()
    reduce_cross.gather_start(1)
    reduce_self.gather_end()
    reduce_self.gather_start(1)

    d_in = rs2_send[0].astype(F32)
    for k in (1, 3, 2):
        rs2_copies[TP - k].wait_recv()
        d_in = d_in + rs2_recv[k - 1].astype(F32)
    normed, inverse = normalize(tok[0].astype(F32))
    dtok_o[...] = (
        grad_own[...] + normalize_back(d_in * (1.0 + per_frame(1, own)), normed, inverse)
    ).astype(BF)
    reduce_cross.gather_end()
    reduce_cross.gather_start(0)

    d_silu = dsil[...]
    for k in range(1, TP):
        arrived(ds_copies, k)
        d_silu = d_silu + dsr[k - 1]
    for item in range(items):
        value = time_ref[item]
        gate = 1.0 / (1.0 + jnp.exp(-value))
        dtime_o[item] = d_silu[item : item + 1, :] * (gate * (1.0 + value * (1.0 - gate)))
    dp_wait(eall.at[dp], eall.at[dp], 0)
    dp_wait(lall.at[dp], lall.at[dp], 1)
    out_copies = [
        pltpu.make_async_copy(eall, early_o, osem.at[3, 0]),
        pltpu.make_async_copy(lall, late_o, osem.at[3, 1]),
    ]
    for copy in out_copies:
        copy.start()
    reduce_self.gather_end()
    reduce_self.gather_start(0)
    for chain in chains:
        chain.finish()
    reduce_cross.gather_end()
    reduce_self.gather_end()
    for copy in pending:
        copy.wait_send()
    for copy in out_copies:
        copy.wait()


def finish_kernel(
    place, items, grads_h, early_ref, late_ref,
    qkv_o, attn_out_o, cross_q_o, cross_kv_o, cross_out_o, up_o, down_o, mod_o,
    gb_attn_o, gb_cross_o, gb_up_o, gb_mod_o,
    low, full_v, kv_v, mod_v, isem, osem,
):
    names = ("up", "down", "qkv", "cross_kv", "attn_out", "cross_out", "cross_q")
    outs = {
        "up": up_o, "down": down_o, "qkv": qkv_o, "attn_out": attn_out_o, "cross_out": cross_out_o,
        "cross_q": cross_q_o, "cross_kv": cross_kv_o,
    }
    loads = {}
    for i, name in enumerate(names):
        at, rows = place[name]
        loads[name] = pltpu.make_async_copy(
            grads_h.at[at : at + rows], low.at[at : at + rows], isem.at[i]
        )
        loads[name].start()
    stores = []

    def store(src, dst, i):
        copy = pltpu.make_async_copy(src, dst, osem.at[i])
        copy.start()
        stores.append(copy)

    dp_count, slots, D = early_ref.shape
    MB = late_ref.shape[2]
    keep = lax.rem(lax.broadcasted_iota(jnp.int32, (dp_count * slots, MB), 0), slots) < items
    late = jnp.where(keep, late_ref[...].reshape(dp_count * slots, MB), 0.0)
    early = early_ref[...]
    mod_v[...] = dot_tn(early.reshape(dp_count * slots, D).astype(BF), late.astype(BF))
    store(mod_v, mod_o, 7)
    gb_mod_o[...] = jnp.sum(late, axis=0)
    sums = jnp.sum(early, axis=0)
    gb_up_o[...] = sums[3]
    gb_cross_o[...] = sums[4]
    gb_attn_o[...] = sums[5]
    for i, name in enumerate(names):
        at, rows = place[name]
        loads[name].wait()
        if name == "cross_kv":
            ident = (
                lax.broadcasted_iota(jnp.int32, (rows, rows), 0)
                == lax.broadcasted_iota(jnp.int32, (rows, rows), 1)
            ).astype(F32).astype(BF)
            kv_v[...] = dot_tn(low[at : at + rows, :], ident)
            store(kv_v, outs[name], i)
        else:
            full_v[at : at + rows, :] = low[at : at + rows, :].astype(F32)
            store(full_v.at[at : at + rows], outs[name], i)
    for copy in stores:
        copy.wait()


def body(
    dp_count,
    tokens,
    seg_ids,
    time_embed,
    text_states,
    text_lengths,
    out_grad,
    w_qkv,
    w_attn_out,
    b_attn_out,
    w_cross_q,
    w_cross_kv,
    w_cross_out,
    b_cross_out,
    w_up,
    b_up,
    w_down,
    w_mod,
    b_mod,
):
    _, R, D = tokens.shape
    T = R * TP
    items = time_embed.shape[1]
    shard_txt = text_states.shape[2]
    TL = items * shard_txt
    TK = TP * TL
    HW = w_cross_q.shape[1]
    HL = HW // DH
    HEADS = TP * HL
    FF = w_up.shape[1]
    MB = w_mod.shape[1]
    place, total_rows = bucket_rows(FF, HW)
    text = text_states[0].reshape(TL, D)

    extra = 0
    step = 8
    while step < dp_count:
        extra += 1
        step *= 2
    room = total_rows - total_rows // 8 + 2 * extra * (total_rows // 16)

    hbm = pl.BlockSpec(memory_space=pl.ANY)
    vmem = pl.BlockSpec(memory_space=pltpu.VMEM)
    smem = pl.BlockSpec(memory_space=pltpu.SMEM)
    V = pltpu.VMEM
    DMA = pltpu.SemaphoreType.DMA
    chunks = max(HL, 2)
    scratch = [
        V((TP, R, D), BF), V((TP, R, D), BF), V((TP, TL, D), BF), V((TP, HW, T), BF), V((TP, R, D), BF),
        V((3 * HW, D), BF), V((D, 2 * HW), BF), V((TP, 5, HW, D), BF),
        V((D, FF), BF), V((FF, D), BF), V((D, MB), BF),
        V((TP, 8, MB), F32), V((6, 8, D), F32), V((1, T), F32), V((T, 1), F32), V((16, T), BF), V((TK, 1), F32),
        V((T, D), BF), V((T, D), BF), V((3 * HW, T), BF), V((2 * HL, T, DH), BF), V((HL, T, T), F32),
        V((T, D), F32), V((T, 1), F32), V((T, D), BF), V((TP * HW, T), BF), V((TP * 2 * HW, TK), BF),
        V((HEADS, TK, DH), BF), V((HEADS, TK, DH), BF), V((HEADS, TK, T), F32), V((TP * HW, T), BF), V((R, D), F32),
        V((T, D), BF), V((R, D), F32), V((R, 1), F32), V((T, FF), BF), V((T, FF), BF), V((T, D), BF),
        V((TP, R, D), BF), V((TP - 1, R, D), BF),
        V((R, D), F32), V((TP * HW, T), BF), V((TP * HW, T), BF), V((TP * 2 * HW, TK), F32),
        V((TP * 2 * HW, TK), BF), V((R, D), F32), V((T, D), BF), V((HW, T), BF), V((3 * HW, T), BF),
        V((2 * DH, T), F32),
        V((TP, R, D), BF), V((TP - 1, R, D), BF),
        V((6, 16, D), F32), V((TP, 8, MB), F32), V((TP - 1, 8, MB), F32), V((8, D), F32), V((TP - 1, 8, D), F32),
        V((8, D), F32), V((dp_count, 8, D), F32), V((dp_count, 8, MB), F32),
        V((total_rows, D), BF), V((room, D), BF),
        DMA((11,)), DMA((5, TP)), DMA((5, TP)), DMA((6, 5, chunks)), DMA((6, TP, chunks)), DMA((4,)), DMA((4,)),
        DMA((3, 2, 6 + extra)), DMA((3, 2, 6 + extra)), DMA((2, dp_count)), DMA((2, dp_count)), DMA((4, 2)),
    ]
    d_tokens, d_time, d_text, grads, early, late = pl.pallas_call(
        functools.partial(layer_kernel, (dp_count, place, items)),
        out_shape=(
            jax.ShapeDtypeStruct((R, D), BF),
            jax.ShapeDtypeStruct((items, 1, D), F32),
            jax.ShapeDtypeStruct((TL, D), BF),
            jax.ShapeDtypeStruct((total_rows, D), BF),
            jax.ShapeDtypeStruct((dp_count, 8, D), F32),
            jax.ShapeDtypeStruct((dp_count, 8, MB), F32),
        ),
        in_specs=[hbm] * 11 + [vmem] * 6 + [smem],
        out_specs=(vmem, vmem, vmem, hbm, hbm, hbm),
        scratch_shapes=scratch,
        name="layer",
        compiler_params=pltpu.CompilerParams(
            collective_id=0, has_side_effects=True, vmem_limit_bytes=63 * 1024 * 1024
        ),
    )(
        tokens[0], out_grad[0], text, w_qkv.T, w_attn_out, w_cross_q.T, w_cross_kv, w_cross_out,
        w_up, w_down, w_mod, seg_ids, jnp.transpose(time_embed, (1, 0, 2)),
        b_attn_out, b_cross_out, b_up, b_mod, text_lengths,
    )

    f32 = lambda *shape: jax.ShapeDtypeStruct(shape, F32)
    g_qkv, g_attn, g_cq, g_ckv, g_co, g_up, g_down, g_mod, gb_attn, gb_cross, gb_up, gb_mod = pl.pallas_call(
        functools.partial(finish_kernel, place, items),
        out_shape=(
            f32(3 * HW, D), f32(HW, D), f32(HW, D), f32(D, 2 * HW), f32(HW, D), f32(FF, D), f32(FF, D),
            f32(D, MB), f32(D), f32(D), f32(FF), f32(MB),
        ),
        in_specs=[hbm, vmem, vmem],
        out_specs=(hbm,) * 8 + (vmem,) * 4,
        scratch_shapes=[
            V((total_rows, D), BF), V((total_rows, D), F32), V((D, 2 * HW), F32), V((D, MB), F32), DMA((7,)), DMA((8,)),
        ],
        name="finish",
        compiler_params=pltpu.CompilerParams(vmem_limit_bytes=40 * 1024 * 1024),
    )(grads, early, late)
    return (
        d_tokens[None],
        jnp.transpose(d_time, (1, 0, 2)),
        d_text.reshape(1, items, shard_txt, D),
        g_qkv.T,
        g_attn,
        gb_attn,
        g_cq.T,
        g_ckv,
        g_co,
        gb_cross,
        g_up,
        gb_up,
        g_down,
        g_mod,
        gb_mod,
    )


def solution(mesh):
    placed = (
        P("dp", "tp", None),
        P("dp", None),
        P("dp", None, None),
        P("dp", None, "tp", None),
        P("dp", None),
        P("dp", "tp", None),
        P(None, "tp"),
        P("tp", None),
        P(),
        P(None, "tp"),
        P(None, "tp"),
        P("tp", None),
        P(),
        P(None, "tp"),
        P("tp"),
        P("tp", None),
        P(None, "tp"),
        P("tp"),
    )
    return jax.shard_map(
        functools.partial(body, mesh.shape["dp"]),
        mesh=mesh,
        in_specs=placed,
        out_specs=(
            P("dp", "tp", None),
            P("dp", None, None),
            P("dp", None, "tp", None),
            P(None, "tp"),
            P("tp", None),
            P(),
            P(None, "tp"),
            P(None, "tp"),
            P("tp", None),
            P(),
            P(None, "tp"),
            P("tp"),
            P("tp", None),
            P(None, "tp"),
            P("tp"),
        ),
        check_vma=False,
    )
```

profile of v0, /device:TPU:1, one launch (start us, length us, event | category | flops | bytes accessed | tf_op | source)
XLA Modules:
  0.0 193.6 jit_solution(2072941054683899421)
XLA Ops:
  0.7 179.7 %layer.1 = (bf16[128,768]{1,0:T(8,128)(2,1)}, f32[3,1,768]{2,1,0:T(1,128)}, bf16[48,768]{1,0:T(8,128)(2,1)}, bf16[3072,768]{1,0:T(8,128)(2,1)}, f32[8,8,768]{2,1,0:T(8,128)}, /*index=5*/f32[8,8,1152]{2,1,0:T(8,128)}) custom-call(bf16[128,768]{1,0:T(8,128)(2,1)} %bitcast.13, bf16[128,768]{1,0:T(8,128)(2,1)} %bitcast.14, bf16[48,768]{1,0:T(8,128)(2,1)} %bitcast.17, ...), custom_call_target="tpu_custom_call" | custom-call | tf_op jit(solution)/shard_map/layer/pallas_call | solution.py:953
  180.4 0.0 copy-start
  180.4 2.3 %copy-done = bf16[3072,768]{1,0:T(8,128)(2,1)S(1)} copy-done((bf16[3072,768]{1,0:T(8,128)(2,1)S(1)}, bf16[3072,768]{1,0:T(8,128)(2,1)}, u32[]{:S(2)}) %copy-start) | copy-done | bytes 4718616
  182.7 0.0 copy-start.1
  182.7 1.0 copy-done.1
  183.7 0.0 copy-start.2
  183.7 0.9 copy-done.2
  184.6 0.0 copy-start.3
  184.6 0.0 copy-start.5
  184.6 0.0 copy-start.4
  184.6 7.0 %finish.1 = (f32[576,768]{1,0:T(8,128)}, f32[192,768]{1,0:T(8,128)}, f32[192,768]{1,0:T(8,128)}, f32[768,384]{1,0:T(8,128)}, f32[192,768]{1,0:T(8,128)}, /*index...) custom-call(bf16[3072,768]{1,0:T(8,128)(2,1)S(1)} %copy-done, ...), custom_call_target="tpu_custom_call" | custom-call | tf_op jit(solution)/shard_map/finish/pallas_call | solution.py:977
  191.7 0.0 copy-done.3
  191.7 0.7 copy.36
  192.4 0.0 copy-done.5
  192.4 0.6 copy.37
  193.0 0.0 copy-done.4
  193.0 0.6 copy.38
Async XLA Ops:
  180.4 2.3 %copy-start = (bf16[3072,768]{1,0:T(8,128)(2,1)S(1)}, bf16[3072,768]{1,0:T(8,128)(2,1)}, u32[]{:S(2)}) copy-start(bf16[3072,768]{1,0:T(8,128)(2,1)} %get-tuple-element.36.grads_h) | copy-start | bytes 14155780
  182.7 1.0 copy-start.1
  183.7 0.9 copy-start.2
  184.6 7.1 %copy-start.3 = (bf16[128,768]{1,0:T(8,128)(2,1)S(1)}, bf16[128,768]{1,0:T(8,128)(2,1)}, u32[]{:S(2)}) copy-start(bf16[128,768]{1,0:T(8,128)(2,1)} %get-tuple-element.33) | copy-start | bytes 589828
  184.6 7.8 %copy-start.5 = (f32[3,1,768]{2,1,0:T(1,128)S(1)}, f32[3,1,768]{2,1,0:T(1,128)}, u32[]{:S(2)}) copy-start(f32[3,1,768]{2,1,0:T(1,128)} %get-tuple-element.34) | copy-start | bytes 27652
  184.6 8.4 %copy-start.4 = (bf16[48,768]{1,0:T(8,128)(2,1)S(1)}, bf16[48,768]{1,0:T(8,128)(2,1)}, u32[]{:S(2)}) copy-start(bf16[48,768]{1,0:T(8,128)(2,1)} %get-tuple-element.35) | copy-start | bytes 221188
where the time goes:
time: 194 us
  Pallas kernels  187 us (96%)
  local copies, waits for them, and re-layouts  6.14 us (3%)
    pallas_call x1, Pallas kernels, body(): pl.pallas_call(functools.partial(layer_kernel, (dp_count, place, items)),...  180 us
    pallas_call x1, Pallas kernels, body(): pl.pallas_call(functools.partial(finish_kernel, place, items), out_shape=...  7.05 us
    unnamed x15, local copies, waits for them, and re-layouts  6.14 us

commit v1 on v0

--- a/solution.py
+++ b/solution.py
@@ -68,9 +68,9 @@
     wqkvT, wckv, wfull, wup, wdn, wmod,
     modbuf, mods, segrow, segcol, onehot, ktag,
     attn_in, na, qkvT, kvx, pself,
-    stream_a, inv_c, cross_in, cqT, ckvT, kx, vx, pcross, catT, branch_own,
-    mlp_in, nm_own, invm_own, act, dpre, dbm, rs_send, rs_recv,
-    gc_own, dcT, dcqT, dckv, dckvT, grad_own, dba, dOT, dqkvT, dkv_acc,
+    stream_a, inv_c, cross_in, cqT, ckvT, kblk, vblk, pcross, catT, branch_own,
+    mlp_in, nm_own, invm_own, act, slope, dpre, dbm, rs_send, rs_recv,
+    gc_own, dcT, dcqT, dckvT, grad_own, dba, dOT, dqkvT,
     rs2_send, rs2_recv, dm, dmp, dmr, dsil, dsr, early, eall, lall,
     grads, rbuf,
     lsem, ssem, rsem, csem_s, csem_r, wsem_s, wsem_r, gsem_s, gsem_r, esem_s, esem_r, osem,
@@ -87,7 +87,6 @@
     TL = text.shape[1]
     HEADS = TP * HL
     MB = modbuf.shape[2]
-    QB = 2 * R
     scale = 1.0 / math.sqrt(DH)
     sub = lax.rem(dp, 8)
     base8 = dp - sub
@@ -212,10 +211,11 @@
     tok_chain = Chain(0, lambda slot, c: tok.at[slot, c * half : (c + 1) * half])
     text_chain = Chain(1, lambda slot, c: text.at[slot])
     WR, WC = HW // 4, D // 2
-    wrow = pl.multiple_of(chip * WR, 16)
     wcol = pl.multiple_of(core * WC, 128)
     pieces = (slice(0, 3), slice(3, 5))
-    w_chain = Chain(2, lambda slot, c: wfull.at[slot, pieces[c], pl.ds(wrow, WR), pl.ds(wcol, WC)])
+    swapped = lax.rem(chip, 2) * 2 + chip // 2
+    places = (chip, swapped)
+    w_chain = Chain(2, lambda slot, c: wfull.at[slot, pieces[c], span(places[c] * WR, WR, 16), pl.ds(wcol, WC)])
     att_chain = Chain(3, lambda slot, c: att.at[slot, c * DH : (c + 1) * DH])
     og_chain = Chain(4, lambda slot, c: og.at[slot, c * half : (c + 1) * half])
     gc_chain = Chain(5, lambda slot, c: gc.at[slot, c * half : (c + 1) * half])
@@ -277,7 +277,7 @@
     def item_sums(rows, values):
         return dot_nn(onehot[:, rows], values.astype(BF))
 
-    own = slice(0, R)
+    own, every = slice(0, R), slice(0, T)
     local[3].wait()
 
     def project(slot):
@@ -289,87 +289,96 @@
         qkvT[:, rows] = dot_nt(wqkvT[...], x).astype(BF)
 
     project(0)
-    for which, slot in enumerate((slot_a, slot_b, slot_c)):
-        tok_chain.step(which, 0)
-        tok_chain.step(which, 1)
-        if which == 0:
-            local[2].wait()
-            local[7].wait()
-            ident = (
-                lax.broadcasted_iota(jnp.int32, (D, D), 0) == lax.broadcasted_iota(jnp.int32, (D, D), 1)
-            ).astype(F32).astype(BF)
-            wckvT = dot_tn(wckv[...], ident).astype(BF)
-            wfull[0, 3] = wckvT[:HW]
-            wfull[0, 4] = wckvT[HW:]
-            for copy in local[4:7]:
-                copy.wait()
-        if which == 2:
-            text_chain.start(0)
-            w_chain.start(0)
-            w_chain.start(1)
-        project(slot)
+    tok_chain.step(0, 0)
+    tok_chain.step(0, 1)
+    local[2].wait()
+    text_chain.start(0)
+    local[7].wait()
+    ident = (
+        lax.broadcasted_iota(jnp.int32, (D, D), 0) == lax.broadcasted_iota(jnp.int32, (D, D), 1)
+    ).astype(F32).astype(BF)
+    wckvT = dot_tn(wckv[...], ident).astype(BF)
+    wfull[0, 3] = wckvT[:HW]
+    wfull[0, 4] = wckvT[HW:]
+    for copy in local[4:7]:
+        copy.wait()
+    tok_chain.step(1, 0)
+    tok_chain.step(1, 1)
+    w_chain.start(0)
+    w_chain.start(1)
+    project(slot_a)
+    text_chain.step(0, 0)
+    tok_chain.step(2, 0)
+    tok_chain.step(2, 1)
+    project(slot_b)
+    w_chain.step(0, 0)
+    project(slot_c)
 
     for h in range(HL):
         q0 = h * 3 * DH
-        keys = (qkvT[q0 + DH : q0 + 2 * DH, :].astype(F32).T * scale).astype(BF)
-        kvx[2 * h] = keys
+        kvx[2 * h] = (qkvT[q0 + DH : q0 + 2 * DH, :].astype(F32).T * scale).astype(BF)
         kvx[2 * h + 1] = qkvT[q0 + 2 * DH : q0 + 3 * DH, :].astype(F32).T.astype(BF)
-
-        def attend(b, carry, h=h, q0=q0):
-            cols = span(b * R, R, R)
-            scores = dot_nn(kvx[2 * h], qkvT[q0 : q0 + DH, cols])
-            scores = jnp.where(segcol[...] == segrow[:, cols], scores, -1000000000.0)
-            peak = jnp.max(scores, axis=0, keepdims=True)
-            exponent = jnp.exp(scores - peak)
-            probs = exponent * (1.0 / jnp.sum(exponent, axis=0, keepdims=True))
-            pself[h, :, cols] = probs
-            att[0, h * DH : (h + 1) * DH, cols] = dot_nn(
-                qkvT[q0 + 2 * DH : q0 + 3 * DH, :], probs.astype(BF)
-            ).astype(BF)
-            return carry
-
-        lax.fori_loop(0, TP, attend, 0)
+        scores = dot_nn(kvx[2 * h], qkvT[q0 : q0 + DH, :])
+        scores = jnp.where(segcol[...] == segrow[...], scores, -1000000000.0)
+        peak = jnp.max(scores, axis=0, keepdims=True)
+        exponent = jnp.exp(scores - peak)
+        probs = exponent * (1.0 / jnp.sum(exponent, axis=0, keepdims=True))
+        pself[h] = probs
+        att[0, h * DH : (h + 1) * DH, :] = dot_nn(qkvT[q0 + 2 * DH : q0 + 3 * DH, :], probs.astype(BF)).astype(BF)
+
+    class Plane:
+        def __init__(self, index, bits):
+            self.index, self.bits, self.open = index, bits, None
+
+        def send(self, step, rows, bit):
+            at = wfull.at[1:TP, pieces[self.index], rows, pl.ds(wcol, WC)]
+            copy = remote(
+                at, at, wsem_s.at[self.index, step], wsem_r.at[self.index, step],
+                {"dp": base8 + jnp.bitwise_xor(sub, bit)},
+            )
+            copy.start()
+            pending.append(copy)
+            self.open = copy
+
+        def step(self, step):
+            if step:
+                self.open.wait_recv()
+            place = places[self.index]
+            if step == 0:
+                self.send(0, span(place * WR, WR, 16), self.bits[0])
+            elif step == 1:
+                self.send(1, span(place // 2 * (2 * WR), 2 * WR, 16), self.bits[1])
+            elif step == 2:
+                self.send(2, slice(0, HW), 1)
+
+    planes = (Plane(0, (2, 4)), Plane(1, (4, 2)))
+    w_chain.step(0, 1)
+    text_chain.step(1, 0)
+    w_chain.step(1, 0)
+    for h in range(HL):
         att_chain.start(h)
-        if h == 0:
-            text_chain.step(0, 0)
-        if h == 1:
-            w_chain.step(0, 0)
-            text_chain.step(1, 0)
-        if h == 2:
-            w_chain.step(0, 1)
-    w_chain.step(1, 0)
     w_chain.step(1, 1)
+    w_chain.step(2, 0)
+    planes[0].step(0)
+    w_chain.step(2, 1)
+    planes[1].step(0)
     text_chain.step(2, 0)
     for h in range(HL):
         att_chain.step(0, h)
-    w_chain.step(2, 0)
-    w_chain.step(2, 1)
     local[8].wait()
-
-    wx = []
-    for m in range(1, 4):
-        peer = {"dp": base8 + jnp.bitwise_xor(sub, 2 * m)}
-        copy = remote(
-            wfull.at[1:TP, :, pl.ds(wrow, WR), pl.ds(wcol, WC)],
-            wfull.at[1:TP, :, pl.ds(wrow, WR), pl.ds(wcol, WC)],
-            wsem_s.at[m], wsem_r.at[m], peer,
-        )
-        copy.start()
-        wx.append(copy)
+    planes[0].step(1)
+    planes[1].step(1)
     for h in range(HL):
         att_chain.step(1, h)
     og_chain.start(0)
     og_chain.start(1)
-    for copy in wx:
-        copy.wait_recv()
-    wlast = remote(
-        wfull.at[1:TP, :, :, pl.ds(wcol, WC)],
-        wfull.at[1:TP, :, :, pl.ds(wcol, WC)],
-        wsem_s.at[0], wsem_r.at[0], {"dp": base8 + jnp.bitwise_xor(sub, 1)},
-    )
-    wlast.start()
-    pending.extend(wx + [wlast])
-    wlast.wait_recv()
+    for h in range(HL):
+        att_chain.step(2, h)
+    planes[0].step(2)
+    planes[1].step(2)
+    og_chain.step(0, 0)
+    og_chain.step(0, 1)
+    planes[1].step(3)
 
     def full(i):
         return wfull[:, i].reshape(TP * HW, D)
@@ -378,110 +387,85 @@
     for s in range(TP):
         for part in range(2):
             ckvT[(2 * s + part) * HW : (2 * s + part + 1) * HW, :] = dot_nt(wfull[s, 3 + part], text_flat).astype(BF)
-    for h in range(HEADS):
-        pair = ckvT[h * 2 * DH : (h + 1) * 2 * DH, :].astype(F32).T
-        kx[h] = (pair[:, :DH] * scale).astype(BF)
-        vx[h] = pair[:, DH:].astype(BF)
-    for h in range(HL):
-        att_chain.step(2, h)
+    quad = 4 * DH
+    lane_head = lax.broadcasted_iota(jnp.int32, (TK, quad), 1) // DH
+    for g in range(HEADS // 4):
+        heads_at = [(4 * g + j) * 2 * DH for j in range(4)]
+        for blocks, offset, factor in ((kblk, 0, scale), (vblk, DH, 1.0)):
+            turned = jnp.concatenate(
+                [ckvT[at + offset : at + offset + DH, :] for at in heads_at], axis=0
+            ).astype(F32).T * factor
+            for j in range(4):
+                blocks[g, j * TK : (j + 1) * TK, :] = jnp.where(lane_head == j, turned, 0.0).astype(BF)
+    og_chain.step(1, 0)
+    og_chain.step(1, 1)
+    planes[0].step(3)
 
     b_attn_out = b_attn_out_ref[...].astype(F32).reshape(1, D)
     b_cross_out = b_cross_out_ref[...].astype(F32).reshape(1, D)
     b_up = b_up_ref[...].astype(F32).reshape(1, wup.shape[1])
 
-    def forward(i, carry):
-        rows = span(i * QB, QB, QB)
-        parts = []
-        for b in range(QB // R):
-            at = i * (QB // R) + b
-            parts.append(
-                jnp.concatenate(
-                    [att[k, :, span(lax.rem(at + TP - k, TP) * R, R, R)] for k in range(TP)], axis=0
-                )
-            )
-        branch = dot_tn(jnp.concatenate(parts, axis=1), full(0)) + b_attn_out
-
-        @pl.when(i == 0)
-        def _():
-            branch_own[...] = branch[:R]
-
-        frames = tok[span(i * (QB // R), QB // R, 1)].reshape(QB, D)
-        stream_a[rows, :] = frames.astype(F32) + per_frame(2, rows) * branch
-        normed, inverse = normalize(stream_a[rows, :])
-        inv_c[rows, :] = inverse
-        x = normed.astype(BF)
-        cross_in[rows, :] = x
-        cqT[:, rows] = dot_nt(full(1), x).astype(BF)
-        allowed = ktag[...] == segrow[:, rows]
-        for h in range(HEADS):
-            hr = slice(h * DH, (h + 1) * DH)
-            scores = dot_nn(kx[h], cqT[hr, rows])
-            scores = jnp.where(allowed, scores, -1000000000.0)
+    gathered = jnp.concatenate(
+        [
+            jnp.concatenate([att[k, :, (b - k) % TP * R : ((b - k) % TP + 1) * R] for b in range(TP)], axis=1)
+            for k in range(TP)
+        ],
+        axis=0,
+    )
+    stream_a[...] = dot_tn(gathered, full(0)) + b_attn_out
+    branch_own[...] = stream_a[own, :]
+    stream_a[...] = tok[...].reshape(T, D).astype(F32) + per_frame(2, every) * stream_a[...]
+    normed, inverse = normalize(stream_a[...])
+    inv_c[...] = inverse
+    cross_in[...] = normed.astype(BF)
+    cqT[...] = dot_nt(full(1), cross_in[...]).astype(BF)
+    allowed = ktag[...] == segrow[...]
+
+    def cross_forward(g, carry):
+        scores_all = dot_nn(kblk[g], cqT[span(g * quad, quad, quad), :])
+        for j in range(4):
+            h = 4 * g + j
+            scores = jnp.where(allowed, scores_all[j * TK : (j + 1) * TK], -1000000000.0)
             peak = jnp.max(scores, axis=0, keepdims=True)
             exponent = jnp.exp(scores - peak)
             probs = exponent * (1.0 / jnp.sum(exponent, axis=0, keepdims=True))
-            pcross[h, :, rows] = probs
-            vT = ckvT[h * 2 * DH + DH : (h + 1) * 2 * DH, :]
-            catT[hr, rows] = dot_nn(vT, probs.astype(BF)).astype(BF)
-        stream = stream_a[rows, :] + dot_tn(catT[:, rows], full(2)) + b_cross_out
-        normed, inverse = normalize(stream)
-
-        @pl.when(i == 0)
-        def _():
-            nm_own[...] = normed[:R]
-            invm_own[...] = inverse[:R]
-
-        mlp_in[rows, :] = (normed * (1.0 + per_frame(4, rows)) + per_frame(3, rows)).astype(BF)
-        for which in range(2):
-
-            @pl.when(i == which)
-            def _():
-                og_chain.step(which, 0)
-                og_chain.step(which, 1)
-
+            pcross[h] = probs
+            vT = ckvT[span(h * 2 * DH + DH, DH, DH), :]
+            catT[span(h * DH, DH, DH), :] = dot_nn(vT, probs.astype(BF)).astype(BF)
         return carry
 
-    lax.fori_loop(0, T // QB, forward, 0)
+    lax.fori_loop(0, HEADS // 4, cross_forward, 0)
     og_chain.step(2, 0)
     og_chain.step(2, 1)
+    normed, inverse = normalize(stream_a[...] + dot_tn(catT[...], full(2)) + b_cross_out)
+    nm_own[...] = normed[:R]
+    invm_own[...] = inverse[:R]
+    mlp_in[...] = (normed * (1.0 + per_frame(4, every)) + per_frame(3, every)).astype(BF)
 
     local[9].wait()
     local[10].wait()
-    dm[5] = jnp.zeros((16, D), F32)
-
-    def rs_copy(b):
-        return remote(
-            rs_send.at[b], rs_recv.at[TP - 1 - b], ssem.at[1, b], rsem.at[1, TP - b], tp_peer(b)
-        )
-
-    def feed(i, carry):
-        b = jnp.where(i == 0, 2, jnp.where(i == 3, 0, 2 * i - 1))
-        rows = span(b * R, R, R)
-        pre = dot_nn(mlp_in[rows, :], wup[...]) + b_up
-        square = pre * pre
-        bend = jnp.tanh(GELU_C * pre * (1.0 + 0.044715 * square))
-        low = (0.5 * pre * (1.0 + bend)).astype(BF)
-        act[rows, :] = low
-        slope = 0.5 * (1.0 + bend) + 0.5 * pre * (1.0 - bend * bend) * (
-            GELU_C * (1.0 + 3.0 * 0.044715 * square)
-        )
-        grad = og[b].astype(F32)
-        d_branch = (grad * per_frame(5, rows)).astype(BF)
-        dbm[rows, :] = d_branch
-        d_pre = (dot_nt(d_branch, wdn[...]) * slope).astype(BF)
-        dpre[rows, :] = d_pre
-        rs_send[b] = dot_nt(d_pre, wup[...]).astype(BF)
-
-        @pl.when(i < 3)
-        def _():
-            rs_copy(b).start()
-
-        dm[5] += item_sums(rows, grad * dot_nn(low, wdn[...]))
-        return carry
-
-    lax.fori_loop(0, TP, feed, 0)
-    rs_copies = {b: rs_copy(b) for b in range(1, TP)}
-    pending.extend(rs_copies.values())
+    pre = dot_nn(mlp_in[...], wup[...]) + b_up
+    square = pre * pre
+    bend = jnp.tanh(GELU_C * pre * (1.0 + 0.044715 * square))
+    act[...] = (0.5 * pre * (1.0 + bend)).astype(BF)
+    slope[...] = 0.5 * (1.0 + bend) + 0.5 * pre * (1.0 - bend * bend) * (
+        GELU_C * (1.0 + 3.0 * 0.044715 * square)
+    )
+    dbm[...] = (og[...].reshape(T, D).astype(F32) * per_frame(5, every)).astype(BF)
+    dpre[...] = (dot_nt(dbm[...], wdn[...]) * slope[...]).astype(BF)
+    rs_send[...] = dot_nt(dpre[...], wup[...]).astype(BF).reshape(TP, R, D)
+
+    def to_owners(source, target, tag):
+        copies = {}
+        for b in (2, 1, 3):
+            copies[b] = remote(
+                source.at[b], target.at[TP - 1 - b], ssem.at[tag, b], rsem.at[tag, TP - b], tp_peer(b)
+            )
+            copies[b].start()
+        pending.extend(copies.values())
+        return copies
+
+    rs_copies = to_owners(rs_send, rs_recv, 1)
     early[3:4, :] = dot_nn(onehot[...], dpre[...])[items : items + 1, :]
 
     bits = []
@@ -595,10 +579,13 @@
     put("up", dot_tn(mlp_in[...], dpre[...]))
     put("down", dot_tn(act[...], dbm[...]))
     reduce_mlp.scatter_start(0)
+    dm[5] = item_sums(every, og[...].reshape(T, D).astype(F32) * dot_nn(act[...], wdn[...]))
 
     d_mlp = rs_send[0].astype(F32)
     reduce_mlp.scatter_end(0)
     reduce_mlp.scatter_start(1)
+    reduce_mlp.scatter_end(1)
+    reduce_mlp.scatter_start(2)
     for k in (1, 3, 2):
         rs_copies[TP - k].wait_recv()
         d_mlp = d_mlp + rs_recv[k - 1].astype(F32)
@@ -611,59 +598,43 @@
     dm[3] = item_sums(own, d_mlp)
     dm[4] = item_sums(own, d_mlp * normed)
 
-    dckv[...] = jnp.zeros(dckv.shape, F32)
-    GROUP = 4
-
-    def backward(slot, first):
-        rows = span(slot * R, R, R)
-        grad_low = gc[slot]
-        dcT[:, rows] = dot_nt(full(2), grad_low).astype(BF)
-
-        def heads(g, carry):
-            for j in range(GROUP):
-                h = g * GROUP + j
-                hr = span(h * DH, DH, DH)
-                kr, vr = span(h * 2 * DH, DH, DH), span(h * 2 * DH + DH, DH, DH)
-                d_out = dcT[hr, rows]
-                probs = pcross[h, :, rows]
-                d_probs = dot_nn(vx[h], d_out)
-                d_scores = (probs * (d_probs - jnp.sum(probs * d_probs, axis=0, keepdims=True))).astype(BF)
-                dcqT[hr, rows] = (dot_nn(ckvT[kr, :], d_scores) * scale).astype(BF)
-                dckv[kr, :] += dot_nt(cqT[hr, rows], d_scores) * scale
-                dckv[vr, :] += dot_nt(d_out, probs.astype(BF))
-            return carry
-
-        lax.fori_loop(0, HEADS // GROUP, heads, 0)
-        d_cross = dot_tn(dcqT[:, rows], full(1))
-        grad = gc_own[...] if first else grad_low.astype(F32)
-        grad = grad + normalize_back(d_cross, cross_in[rows, :].astype(F32), inv_c[rows, :])
-        if first:
-            grad_own[...] = grad
-            dm[2] = item_sums(own, grad * branch_own[...])
-        low = (grad * per_frame(2, rows)).astype(BF)
-        dba[rows, :] = low
-        dOT[:, rows] = dot_nt(wfull[0, 0], low).astype(BF)
-
-    backward(0, True)
-    gc_chain.step(0, 0)
-    gc_chain.step(0, 1)
-    gc_chain.step(1, 0)
-    gc_chain.step(1, 1)
-    reduce_mlp.scatter_end(1)
-    reduce_mlp.scatter_start(2)
-    backward(slot_a, False)
-    gc_chain.step(2, 0)
-    gc_chain.step(2, 1)
     reduce_mlp.scatter_end(2)
     reduce_mlp.widen()
     reduce_mlp.gather_start(2)
-    backward(slot_b, False)
-    reduce_mlp.gather_end()
-    reduce_mlp.gather_start(1)
-    backward(slot_c, False)
-
+    for which in range(3):
+        gc_chain.step(which, 0)
+        gc_chain.step(which, 1)
+        if which == 1:
+            reduce_mlp.gather_end()
+            reduce_mlp.gather_start(1)
     gc_flat = gc[...].reshape(T, D)
-    dckvT[...] = dckv[...].astype(BF)
+    dcT[...] = dot_nt(full(2), gc_flat).astype(BF)
+
+    def cross_backward(g, carry):
+        d_probs_all = dot_nn(vblk[g], dcT[span(g * quad, quad, quad), :])
+        for j in range(4):
+            h = 4 * g + j
+            hr = span(h * DH, DH, DH)
+            kr, vr = span(h * 2 * DH, DH, DH), span(h * 2 * DH + DH, DH, DH)
+            probs = pcross[h]
+            d_probs = d_probs_all[j * TK : (j + 1) * TK]
+            d_scores = (probs * (d_probs - jnp.sum(probs * d_probs, axis=0, keepdims=True))).astype(BF)
+            dcqT[hr, :] = (dot_nn(ckvT[kr, :], d_scores) * scale).astype(BF)
+            dckvT[kr, :] = (dot_nt(cqT[hr, :], d_scores) * scale).astype(BF)
+            dckvT[vr, :] = dot_nt(dcT[hr, :], probs.astype(BF)).astype(BF)
+        return carry
+
+    lax.fori_loop(0, HEADS // 4, cross_backward, 0)
+    d_cross = dot_tn(dcqT[...], full(1))
+    back = normalize_back(d_cross, cross_in[...].astype(F32), inv_c[...])
+    grad = gc_own[...] + back[:R]
+    grad_own[...] = grad
+    gate = per_frame(2, every)
+    dba[own, :] = (grad * gate[:R]).astype(BF)
+    rest = slice(R, T)
+    dba[rest, :] = ((gc_flat[R:].astype(F32) + back[R:]) * gate[R:]).astype(BF)
+    dOT[...] = dot_nt(wfull[0, 0], dba[...]).astype(BF)
+
     put("cross_out", dot_nn(catT[0:HW, :], gc_flat))
     put("cross_q", dot_nn(dcqT[0:HW, :], cross_in[...]))
     put("cross_kv", dot_nn(dckvT[0 : 2 * HW, :], text_flat))
@@ -697,55 +668,24 @@
     for h in range(HL):
         q0 = h * 3 * DH
         hr = slice(h * DH, (h + 1) * DH)
-        dkv_acc[...] = jnp.zeros(dkv_acc.shape, F32)
-
-        def attend_back(b, carry, h=h, q0=q0, hr=hr):
-            cols = span(b * R, R, R)
-            d_out = dOT[hr, cols]
-            probs = pself[h, :, cols]
-            d_probs = dot_nn(kvx[2 * h + 1], d_out)
-            d_scores = (probs * (d_probs - jnp.sum(probs * d_probs, axis=0, keepdims=True))).astype(BF)
-            dqkvT[q0 : q0 + DH, cols] = (dot_nn(qkvT[q0 + DH : q0 + 2 * DH, :], d_scores) * scale).astype(BF)
-            dkv_acc[0:DH, :] += dot_nt(qkvT[q0 : q0 + DH, cols], d_scores) * scale
-            dkv_acc[DH : 2 * DH, :] += dot_nt(d_out, probs.astype(BF))
-            return carry
-
-        lax.fori_loop(0, TP, attend_back, 0)
-        dqkvT[q0 + DH : q0 + 3 * DH, :] = dkv_acc[...].astype(BF)
-        if h == 0:
-            reduce_cross.scatter_end(0)
-            reduce_cross.scatter_start(1)
-            reduce_mlp.gather_end()
-            reduce_mlp.gather_start(0)
-
-    dm[0] = jnp.zeros((16, D), F32)
-    dm[1] = jnp.zeros((16, D), F32)
-
-    def rs2_copy(b):
-        return remote(
-            rs2_send.at[b], rs2_recv.at[TP - 1 - b], ssem.at[2, b], rsem.at[2, TP - b], tp_peer(b)
-        )
-
-    def entry(i, carry):
-        b = jnp.where(i == 0, 2, jnp.where(i == 3, 0, 2 * i - 1))
-        rows = span(b * R, R, R)
-        part = dot_tn(dqkvT[:, rows], wqkvT[...])
-        rs2_send[b] = part.astype(BF)
-
-        @pl.when(i < 3)
-        def _():
-            rs2_copy(b).start()
-
-        dm[0] += item_sums(rows, part)
-        dm[1] += item_sums(rows, part * na[rows, :].astype(F32))
-        return carry
-
-    lax.fori_loop(0, TP, entry, 0)
-    rs2_copies = {b: rs2_copy(b) for b in range(1, TP)}
-    pending.extend(rs2_copies.values())
+        probs = pself[h]
+        d_probs = dot_nn(kvx[2 * h + 1], dOT[hr, :])
+        d_scores = (probs * (d_probs - jnp.sum(probs * d_probs, axis=0, keepdims=True))).astype(BF)
+        dqkvT[q0 : q0 + DH, :] = (dot_nn(qkvT[q0 + DH : q0 + 2 * DH, :], d_scores) * scale).astype(BF)
+        dqkvT[q0 + DH : q0 + 2 * DH, :] = (dot_nt(qkvT[q0 : q0 + DH, :], d_scores) * scale).astype(BF)
+        dqkvT[q0 + 2 * DH : q0 + 3 * DH, :] = dot_nt(dOT[hr, :], probs.astype(BF)).astype(BF)
 
     put("qkv", dot_nn(dqkvT[...], attn_in[...]))
     reduce_self.scatter_start(0)
+    reduce_cross.scatter_end(0)
+    reduce_cross.scatter_start(1)
+
+    part = dot_tn(dqkvT[...], wqkvT[...])
+    rs2_send[...] = part.astype(BF).reshape(TP, R, D)
+    input_grad = rs2_send[...].reshape(T, D)
+    dm[0] = dot_nn(onehot[...], input_grad)
+    dm[1] = item_sums(every, input_grad.astype(F32) * na[...].astype(F32))
+    dm[2] = item_sums(own, grad_own[...] * branch_own[...])
 
     for j in range(6):
         lo, hi = j * D, (j + 1) * D
@@ -758,12 +698,15 @@
     dm_copies = direct(
         3, lambda k: dmp.at[lax.rem(tp + k, TP)], lambda k: dmr.at[TP - 1 - k]
     )
+    rs2_copies = to_owners(rs2_send, rs2_recv, 2)
     reduce_self.scatter_end(0)
     reduce_self.scatter_start(1)
+    reduce_mlp.gather_end()
+    reduce_mlp.gather_start(0)
+
+    dtext_o[...] = dot_tn(dckvT[:, 0:TL], wfull[:, 3:5].reshape(TP * 2 * HW, D)).astype(BF)
     reduce_cross.scatter_end(1)
     reduce_cross.scatter_start(2)
-
-    dtext_o[...] = dot_tn(dckvT[:, 0:TL], wfull[:, 3:5].reshape(TP * 2 * HW, D)).astype(BF)
 
     d_mod = dmp[tp]
     for k in range(1, TP):
@@ -771,19 +714,19 @@
         d_mod = d_mod + dmr[k - 1]
     low = d_mod.astype(BF)
     lall[dp] = low.astype(F32)
-    dp_send(lall.at[dp], lall.at[dp], 1)
     dsil[...] = dot_nt(low, wmod[...])
     ds_copies = direct(4, lambda k: dsil, lambda k: dsr.at[TP - 1 - k])
 
     reduce_self.scatter_end(1)
     reduce_self.scatter_start(2)
+    dp_send(lall.at[dp], lall.at[dp], 1)
     reduce_cross.scatter_end(2)
     reduce_cross.widen()
     reduce_cross.gather_start(2)
-    reduce_mlp.gather_end()
     reduce_self.scatter_end(2)
     reduce_self.widen()
     reduce_self.gather_start(2)
+    reduce_mlp.gather_end()
     reduce_cross.gather_end()
     reduce_cross.gather_start(1)
     reduce_self.gather_end()
@@ -829,10 +772,10 @@
 
 
 def finish_kernel(
-    place, items, grads_h, early_ref, late_ref,
-    qkv_o, attn_out_o, cross_q_o, cross_kv_o, cross_out_o, up_o, down_o, mod_o,
+    place, items, grads_h, early_h, late_h, dtok_h, dtime_h, dtext_h,
+    dtok_o, dtime_o, dtext_o, qkv_o, attn_out_o, cross_q_o, cross_kv_o, cross_out_o, up_o, down_o, mod_o,
     gb_attn_o, gb_cross_o, gb_up_o, gb_mod_o,
-    low, full_v, kv_v, mod_v, isem, osem,
+    low, full_v, kv_v, mod_v, early_v, late_v, isem, osem,
 ):
     names = ("up", "down", "qkv", "cross_kv", "attn_out", "cross_out", "cross_q")
     outs = {
@@ -840,24 +783,36 @@
         "cross_q": cross_q_o, "cross_kv": cross_kv_o,
     }
     loads = {}
+    small = [
+        pltpu.make_async_copy(early_h, early_v, isem.at[7]),
+        pltpu.make_async_copy(late_h, late_v, isem.at[8]),
+    ]
+    stores = [
+        pltpu.make_async_copy(dtok_h, dtok_o, osem.at[8]),
+        pltpu.make_async_copy(dtime_h, dtime_o, osem.at[9]),
+        pltpu.make_async_copy(dtext_h, dtext_o, osem.at[10]),
+    ]
+    for copy in small + stores:
+        copy.start()
     for i, name in enumerate(names):
         at, rows = place[name]
         loads[name] = pltpu.make_async_copy(
             grads_h.at[at : at + rows], low.at[at : at + rows], isem.at[i]
         )
         loads[name].start()
-    stores = []
 
     def store(src, dst, i):
         copy = pltpu.make_async_copy(src, dst, osem.at[i])
         copy.start()
         stores.append(copy)
 
-    dp_count, slots, D = early_ref.shape
-    MB = late_ref.shape[2]
+    dp_count, slots, D = early_v.shape
+    MB = late_v.shape[2]
+    for copy in small:
+        copy.wait()
     keep = lax.rem(lax.broadcasted_iota(jnp.int32, (dp_count * slots, MB), 0), slots) < items
-    late = jnp.where(keep, late_ref[...].reshape(dp_count * slots, MB), 0.0)
-    early = early_ref[...]
+    late = jnp.where(keep, late_v[...].reshape(dp_count * slots, MB), 0.0)
+    early = early_v[...]
     mod_v[...] = dot_tn(early.reshape(dp_count * slots, D).astype(BF), late.astype(BF))
     store(mod_v, mod_o, 7)
     gb_mod_o[...] = jnp.sum(late, axis=0)
@@ -937,17 +892,16 @@
         V((TP, 8, MB), F32), V((6, 8, D), F32), V((1, T), F32), V((T, 1), F32), V((16, T), BF), V((TK, 1), F32),
         V((T, D), BF), V((T, D), BF), V((3 * HW, T), BF), V((2 * HL, T, DH), BF), V((HL, T, T), F32),
         V((T, D), F32), V((T, 1), F32), V((T, D), BF), V((TP * HW, T), BF), V((TP * 2 * HW, TK), BF),
-        V((HEADS, TK, DH), BF), V((HEADS, TK, DH), BF), V((HEADS, TK, T), F32), V((TP * HW, T), BF), V((R, D), F32),
-        V((T, D), BF), V((R, D), F32), V((R, 1), F32), V((T, FF), BF), V((T, FF), BF), V((T, D), BF),
+        V((HEADS // 4, 4 * TK, 4 * DH), BF), V((HEADS // 4, 4 * TK, 4 * DH), BF), V((HEADS, TK, T), F32), V((TP * HW, T), BF), V((R, D), F32),
+        V((T, D), BF), V((R, D), F32), V((R, 1), F32), V((T, FF), BF), V((T, FF), F32), V((T, FF), BF), V((T, D), BF),
         V((TP, R, D), BF), V((TP - 1, R, D), BF),
-        V((R, D), F32), V((TP * HW, T), BF), V((TP * HW, T), BF), V((TP * 2 * HW, TK), F32),
+        V((R, D), F32), V((TP * HW, T), BF), V((TP * HW, T), BF),
         V((TP * 2 * HW, TK), BF), V((R, D), F32), V((T, D), BF), V((HW, T), BF), V((3 * HW, T), BF),
-        V((2 * DH, T), F32),
         V((TP, R, D), BF), V((TP - 1, R, D), BF),
         V((6, 16, D), F32), V((TP, 8, MB), F32), V((TP - 1, 8, MB), F32), V((8, D), F32), V((TP - 1, 8, D), F32),
         V((8, D), F32), V((dp_count, 8, D), F32), V((dp_count, 8, MB), F32),
         V((total_rows, D), BF), V((room, D), BF),
-        DMA((11,)), DMA((5, TP)), DMA((5, TP)), DMA((6, 5, chunks)), DMA((6, TP, chunks)), DMA((4,)), DMA((4,)),
+        DMA((11,)), DMA((5, TP)), DMA((5, TP)), DMA((6, 5, chunks)), DMA((6, TP, chunks)), DMA((2, 3)), DMA((2, 3)),
         DMA((3, 2, 6 + extra)), DMA((3, 2, 6 + extra)), DMA((2, dp_count)), DMA((2, dp_count)), DMA((4, 2)),
     ]
     d_tokens, d_time, d_text, grads, early, late = pl.pallas_call(
@@ -974,20 +928,22 @@
     )
 
     f32 = lambda *shape: jax.ShapeDtypeStruct(shape, F32)
-    g_qkv, g_attn, g_cq, g_ckv, g_co, g_up, g_down, g_mod, gb_attn, gb_cross, gb_up, gb_mod = pl.pallas_call(
+    d_tokens, d_time, d_text, g_qkv, g_attn, g_cq, g_ckv, g_co, g_up, g_down, g_mod, gb_attn, gb_cross, gb_up, gb_mod = pl.pallas_call(
         functools.partial(finish_kernel, place, items),
         out_shape=(
+            jax.ShapeDtypeStruct((R, D), BF), f32(items, 1, D), jax.ShapeDtypeStruct((TL, D), BF),
             f32(3 * HW, D), f32(HW, D), f32(HW, D), f32(D, 2 * HW), f32(HW, D), f32(FF, D), f32(FF, D),
             f32(D, MB), f32(D), f32(D), f32(FF), f32(MB),
         ),
-        in_specs=[hbm, vmem, vmem],
-        out_specs=(hbm,) * 8 + (vmem,) * 4,
+        in_specs=[hbm] * 6,
+        out_specs=(hbm,) * 11 + (vmem,) * 4,
         scratch_shapes=[
-            V((total_rows, D), BF), V((total_rows, D), F32), V((D, 2 * HW), F32), V((D, MB), F32), DMA((7,)), DMA((8,)),
+            V((total_rows, D), BF), V((total_rows, D), F32), V((D, 2 * HW), F32), V((D, MB), F32),
+            V((dp_count, 8, D), F32), V((dp_count, 8, MB), F32), DMA((9,)), DMA((11,)),
         ],
         name="finish",
-        compiler_params=pltpu.CompilerParams(vmem_limit_bytes=40 * 1024 * 1024),
-    )(grads, early, late)
+        compiler_params=pltpu.CompilerParams(vmem_limit_bytes=63 * 1024 * 1024),
+    )(grads, early, late, d_tokens, d_time, d_text)
     return (
         d_tokens[None],
         jnp.transpose(d_time, (1, 0, 2)),

time: 194 us -> 161 us (0.83)
  Pallas kernels: 187 us -> 160 us
  local copies, waits for them, and re-layouts: 6.14 us -> 0 us
    pallas_call x1, Pallas kernels: 180 us -> 150 us  [body(): pl.pallas_call(functools.partial(layer_kernel, (dp_count, place, items)),...]
    unnamed x15 -> x0, local copies, waits for them, and re-layouts: 6.14 us -> none
    pallas_call x1, Pallas kernels: 7.05 us -> 10.4 us  [body(): pl.pallas_call(functools.partial(finish_kernel, place, items), out_shape=...]
where the time goes in v1:
time: 161 us
  Pallas kernels  160 us (99%)
    pallas_call x1, Pallas kernels, body(): pl.pallas_call(functools.partial(layer_kernel, (dp_count, place, items)),...  150 us
    pallas_call x1, Pallas kernels, body(): pl.pallas_call(functools.partial(finish_kernel, place, items), out_shape=...  10.4 us

profile of v1, /device:TPU:1, one launch (start us, length us, event | category | flops | bytes accessed | tf_op | source)
XLA Modules:
  0.0 161.1 jit_solution(9466695400414077050)
XLA Ops:
  0.7 149.9 %layer.1 = (bf16[128,768]{1,0:T(8,128)(2,1)}, f32[3,1,768]{2,1,0:T(1,128)}, bf16[48,768]{1,0:T(8,128)(2,1)}, bf16[3072,768]{1,0:T(8,128)(2,1)}, f32[8,8,768]{2,1,0:T(8,128)}, /*index=5*/f32[8,8,1152]{2,1,0:T(8,128)}) custom-call(bf16[128,768]{1,0:T(8,128)(2,1)} %bitcast.13, bf16[128,768]{1,0:T(8,128)(2,1)} %bitcast.14, bf16[48,768]{1,0:T(8,128)(2,1)} %bitcast.15, ...), custom_call_target="tpu_custom_call" | custom-call | tf_op jit(solution)/shard_map/layer/pallas_call | solution.py:907
  150.6 10.4 %finish.1 = (bf16[128,768]{1,0:T(8,128)(2,1)}, f32[3,1,768]{2,1,0:T(1,128)}, bf16[48,768]{1,0:T(8,128)(2,1)}, f32[576,768]{1,0:T(8,128)}, f32[192,768]{1,0:T(8,1...) custom-call(bf16[3072,768]{1,0:T(8,128)(2,1)} %get-tuple-element.36., ...), custom_call_target="tpu_custom_call" | custom-call | tf_op jit(solution)/shard_map/finish/pallas_call | solution.py:931

commit v2 on v1

--- a/solution.py
+++ b/solution.py
@@ -105,14 +105,14 @@
         return pl.ds(pl.multiple_of(at, unit), size)
 
     loads = [
+        (wckv_h, wckv),
+        (wo_h, wfull.at[0, 0]),
+        (wcqT_h, wfull.at[0, 1]),
+        (wco_h, wfull.at[0, 2]),
         (tok_h, tok.at[0]),
         (wmod_h, wmod),
+        (wqkvT_h, wqkvT),
         (text_h, text.at[0]),
-        (wqkvT_h, wqkvT),
-        (wcqT_h, wfull.at[0, 1]),
-        (wo_h, wfull.at[0, 0]),
-        (wco_h, wfull.at[0, 2]),
-        (wckv_h, wckv),
         (og_h, og.at[0]),
         (wup_h, wup),
         (wdn_h, wdn),
@@ -140,9 +140,17 @@
     sig = 1.0 / (1.0 + jnp.exp(-time))
     silu_low = (time * sig).astype(BF)
     early[...] = silu_low.astype(F32)
-    local[1].wait()
+    local[5].wait()
     modbuf[tp] = dot_nn(silu_low, wmod[...]) + b_mod_ref[...].astype(F32).reshape(1, MB)
     local[0].wait()
+    ident = (
+        lax.broadcasted_iota(jnp.int32, (D, D), 0) == lax.broadcasted_iota(jnp.int32, (D, D), 1)
+    ).astype(F32).astype(BF)
+    wckvT = dot_tn(wckv[...], ident).astype(BF)
+    wfull[0, 3] = wckvT[:HW]
+    wfull[0, 4] = wckvT[HW:]
+    for copy in local[1:5]:
+        copy.wait()
 
     pl.semaphore_wait(barrier, TP - 1 + dp_count - 1)
 
@@ -212,13 +220,40 @@
     text_chain = Chain(1, lambda slot, c: text.at[slot])
     WR, WC = HW // 4, D // 2
     wcol = pl.multiple_of(core * WC, 128)
-    pieces = (slice(0, 3), slice(3, 5))
+    mats = (3, 4, 0, 1, 2)
     swapped = lax.rem(chip, 2) * 2 + chip // 2
-    places = (chip, swapped)
-    w_chain = Chain(2, lambda slot, c: wfull.at[slot, pieces[c], span(places[c] * WR, WR, 16), pl.ds(wcol, WC)])
+    places = (chip, swapped, chip, swapped, chip)
+    w_chain = Chain(2, lambda slot, c: wfull.at[slot, mats[c], span(places[c] * WR, WR, 16), pl.ds(wcol, WC)])
     att_chain = Chain(3, lambda slot, c: att.at[slot, c * DH : (c + 1) * DH])
     og_chain = Chain(4, lambda slot, c: og.at[slot, c * half : (c + 1) * half])
     gc_chain = Chain(5, lambda slot, c: gc.at[slot, c * half : (c + 1) * half])
+
+    class Plane:
+        def __init__(self, index, bits):
+            self.index, self.bits, self.open = index, bits, None
+
+        def send(self, step, rows, bit):
+            at = wfull.at[1:TP, mats[self.index], rows, pl.ds(wcol, WC)]
+            copy = remote(
+                at, at, wsem_s.at[self.index, step], wsem_r.at[self.index, step],
+                {"dp": base8 + jnp.bitwise_xor(sub, bit)},
+            )
+            copy.start()
+            pending.append(copy)
+            self.open = copy
+
+        def step(self, step):
+            if step:
+                self.open.wait_recv()
+            place = places[self.index]
+            if step == 0:
+                self.send(0, span(place * WR, WR, 16), self.bits[0])
+            elif step == 1:
+                self.send(1, span(place // 2 * (2 * WR), 2 * WR, 16), self.bits[1])
+            elif step == 2:
+                self.send(2, slice(0, HW), 1)
+
+    planes = [Plane(i, (4, 2) if i % 2 else (2, 4)) for i in range(5)]
 
     def direct(tag, src_of, dst_of):
         copies = []
@@ -232,9 +267,11 @@
     def arrived(copies, slot):
         copies[TP - 1 - slot].wait_recv()
 
+    w_chain.start(0)
+    w_chain.start(1)
     tok_chain.start(0)
     tok_chain.start(1)
-    mod_copies = direct(0, lambda k: modbuf.at[tp], lambda k: modbuf.at[tp])
+    mod_copies = direct(0, lambda k: modbuf.at[tp, 0:items], lambda k: modbuf.at[tp, 0:items])
 
     eye = lax.broadcasted_iota(jnp.int32, (R, R), 0) == lax.broadcasted_iota(jnp.int32, (R, R), 1)
     for slot in range(TP):
@@ -264,7 +301,7 @@
         while at < hi:
             block = at // MB
             end = min(hi, (block + 1) * MB)
-            mods[j, :, at - lo : end - lo] = modbuf[block, :, at - block * MB : end - block * MB]
+            mods[j, 0:items, at - lo : end - lo] = modbuf[block, 0:items, at - block * MB : end - block * MB]
             at = end
 
     def per_frame(j, rows):
@@ -278,7 +315,7 @@
         return dot_nn(onehot[:, rows], values.astype(BF))
 
     own, every = slice(0, R), slice(0, T)
-    local[3].wait()
+    local[6].wait()
 
     def project(slot):
         rows = span(slot * R, R, R)
@@ -288,31 +325,36 @@
         attn_in[rows, :] = x
         qkvT[:, rows] = dot_nt(wqkvT[...], x).astype(BF)
 
+    def w_step(which, *chunks):
+        for chunk in chunks:
+            w_chain.step(which, chunk)
+            if which == 2:
+                planes[chunk].step(0)
+
     project(0)
+    w_step(0, 0, 1)
     tok_chain.step(0, 0)
     tok_chain.step(0, 1)
-    local[2].wait()
+    for chunk in (2, 3, 4):
+        w_chain.start(chunk)
+    local[7].wait()
     text_chain.start(0)
-    local[7].wait()
-    ident = (
-        lax.broadcasted_iota(jnp.int32, (D, D), 0) == lax.broadcasted_iota(jnp.int32, (D, D), 1)
-    ).astype(F32).astype(BF)
-    wckvT = dot_tn(wckv[...], ident).astype(BF)
-    wfull[0, 3] = wckvT[:HW]
-    wfull[0, 4] = wckvT[HW:]
-    for copy in local[4:7]:
-        copy.wait()
+    w_step(1, 0, 1)
     tok_chain.step(1, 0)
     tok_chain.step(1, 1)
-    w_chain.start(0)
-    w_chain.start(1)
+    w_step(2, 0, 1)
     project(slot_a)
-    text_chain.step(0, 0)
+    w_step(0, 2, 3, 4)
+    planes[0].step(1)
+    planes[1].step(1)
+    project(slot_b)
     tok_chain.step(2, 0)
     tok_chain.step(2, 1)
-    project(slot_b)
-    w_chain.step(0, 0)
+    text_chain.step(0, 0)
+    w_step(1, 2, 3, 4)
     project(slot_c)
+    planes[0].step(2)
+    planes[1].step(2)
 
     for h in range(HL):
         q0 = h * 3 * DH
@@ -326,59 +368,15 @@
         pself[h] = probs
         att[0, h * DH : (h + 1) * DH, :] = dot_nn(qkvT[q0 + 2 * DH : q0 + 3 * DH, :], probs.astype(BF)).astype(BF)
 
-    class Plane:
-        def __init__(self, index, bits):
-            self.index, self.bits, self.open = index, bits, None
-
-        def send(self, step, rows, bit):
-            at = wfull.at[1:TP, pieces[self.index], rows, pl.ds(wcol, WC)]
-            copy = remote(
-                at, at, wsem_s.at[self.index, step], wsem_r.at[self.index, step],
-                {"dp": base8 + jnp.bitwise_xor(sub, bit)},
-            )
-            copy.start()
-            pending.append(copy)
-            self.open = copy
-
-        def step(self, step):
-            if step:
-                self.open.wait_recv()
-            place = places[self.index]
-            if step == 0:
-                self.send(0, span(place * WR, WR, 16), self.bits[0])
-            elif step == 1:
-                self.send(1, span(place // 2 * (2 * WR), 2 * WR, 16), self.bits[1])
-            elif step == 2:
-                self.send(2, slice(0, HW), 1)
-
-    planes = (Plane(0, (2, 4)), Plane(1, (4, 2)))
-    w_chain.step(0, 1)
-    text_chain.step(1, 0)
-    w_chain.step(1, 0)
     for h in range(HL):
         att_chain.start(h)
-    w_chain.step(1, 1)
-    w_chain.step(2, 0)
-    planes[0].step(0)
-    w_chain.step(2, 1)
-    planes[1].step(0)
+    w_step(2, 2, 3, 4)
+    text_chain.step(1, 0)
     text_chain.step(2, 0)
-    for h in range(HL):
-        att_chain.step(0, h)
-    local[8].wait()
-    planes[0].step(1)
-    planes[1].step(1)
-    for h in range(HL):
-        att_chain.step(1, h)
-    og_chain.start(0)
-    og_chain.start(1)
-    for h in range(HL):
-        att_chain.step(2, h)
-    planes[0].step(2)
-    planes[1].step(2)
-    og_chain.step(0, 0)
-    og_chain.step(0, 1)
+    planes[0].step(3)
     planes[1].step(3)
+    planes[2].step(1)
+    planes[3].step(1)
 
     def full(i):
         return wfull[:, i].reshape(TP * HW, D)
@@ -397,9 +395,23 @@
             ).astype(F32).T * factor
             for j in range(4):
                 blocks[g, j * TK : (j + 1) * TK, :] = jnp.where(lane_head == j, turned, 0.0).astype(BF)
-    og_chain.step(1, 0)
-    og_chain.step(1, 1)
-    planes[0].step(3)
+    planes[4].step(1)
+    for h in range(HL):
+        att_chain.step(0, h)
+    planes[2].step(2)
+    planes[3].step(2)
+    for h in range(HL):
+        att_chain.step(1, h)
+    local[8].wait()
+    og_chain.start(0)
+    og_chain.start(1)
+    planes[4].step(2)
+    for h in range(HL):
+        att_chain.step(2, h)
+    for plane in planes[2:]:
+        plane.step(3)
+    og_chain.step(0, 0)
+    og_chain.step(0, 1)
 
     b_attn_out = b_attn_out_ref[...].astype(F32).reshape(1, D)
     b_cross_out = b_cross_out_ref[...].astype(F32).reshape(1, D)
@@ -420,6 +432,8 @@
     cross_in[...] = normed.astype(BF)
     cqT[...] = dot_nt(full(1), cross_in[...]).astype(BF)
     allowed = ktag[...] == segrow[...]
+    og_chain.step(1, 0)
+    og_chain.step(1, 1)
 
     def cross_forward(g, carry):
         scores_all = dot_nn(kblk[g], cqT[span(g * quad, quad, quad), :])
@@ -455,17 +469,17 @@
     dpre[...] = (dot_nt(dbm[...], wdn[...]) * slope[...]).astype(BF)
     rs_send[...] = dot_nt(dpre[...], wup[...]).astype(BF).reshape(TP, R, D)
 
-    def to_owners(source, target, tag):
+    def to_owners(source, target, tag, rows):
         copies = {}
         for b in (2, 1, 3):
             copies[b] = remote(
-                source.at[b], target.at[TP - 1 - b], ssem.at[tag, b], rsem.at[tag, TP - b], tp_peer(b)
+                source.at[b, rows], target.at[TP - 1 - b, rows], ssem.at[tag, b], rsem.at[tag, TP - b], tp_peer(b)
             )
             copies[b].start()
-        pending.extend(copies.values())
         return copies
 
-    rs_copies = to_owners(rs_send, rs_recv, 1)
+    halves = (slice(0, half), slice(half, R))
+    rs_first = to_owners(rs_send, rs_recv, 1, halves[0])
     early[3:4, :] = dot_nn(onehot[...], dpre[...])[items : items + 1, :]
 
     bits = []
@@ -581,32 +595,46 @@
     reduce_mlp.scatter_start(0)
     dm[5] = item_sums(every, og[...].reshape(T, D).astype(F32) * dot_nn(act[...], wdn[...]))
 
-    d_mlp = rs_send[0].astype(F32)
     reduce_mlp.scatter_end(0)
     reduce_mlp.scatter_start(1)
+    for copy in rs_first.values():
+        copy.wait_send()
+    rs_second = to_owners(rs_send, rs_recv, 5, halves[1])
+    pending.extend(rs_second.values())
+
+    def stream_grad(chunk, copies):
+        rows = halves[chunk]
+        d_mlp = rs_send[0, rows].astype(F32)
+        for k in (1, 3, 2):
+            copies[TP - k].wait_recv()
+            d_mlp = d_mlp + rs_recv[k - 1, rows].astype(F32)
+        grad_c = og[0, rows].astype(F32) + normalize_back(
+            d_mlp * (1.0 + per_frame(4, rows)), nm_own[rows, :], invm_own[rows, :]
+        )
+        gc_own[rows, :] = grad_c
+        gc[0, rows] = grad_c.astype(BF)
+        gc_chain.start(chunk)
+        return d_mlp
+
+    first = stream_grad(0, rs_first)
     reduce_mlp.scatter_end(1)
     reduce_mlp.scatter_start(2)
-    for k in (1, 3, 2):
-        rs_copies[TP - k].wait_recv()
-        d_mlp = d_mlp + rs_recv[k - 1].astype(F32)
-    normed = nm_own[...]
-    grad_c = og[0].astype(F32) + normalize_back(d_mlp * (1.0 + per_frame(4, own)), normed, invm_own[...])
-    gc_own[...] = grad_c
-    gc[0] = grad_c.astype(BF)
-    gc_chain.start(0)
-    gc_chain.start(1)
-    dm[3] = item_sums(own, d_mlp)
-    dm[4] = item_sums(own, d_mlp * normed)
-
+    gc_chain.step(0, 0)
+    second = stream_grad(1, rs_second)
+    gc_chain.step(1, 0)
     reduce_mlp.scatter_end(2)
     reduce_mlp.widen()
     reduce_mlp.gather_start(2)
-    for which in range(3):
-        gc_chain.step(which, 0)
-        gc_chain.step(which, 1)
-        if which == 1:
-            reduce_mlp.gather_end()
-            reduce_mlp.gather_start(1)
+    d_mlp = jnp.concatenate([first, second], axis=0)
+    dm[3] = item_sums(own, d_mlp)
+    dm[4] = item_sums(own, d_mlp * nm_own[...])
+    gc_chain.step(2, 0)
+
+    gc_chain.step(0, 1)
+    gc_chain.step(1, 1)
+    reduce_mlp.gather_end()
+    reduce_mlp.gather_start(1)
+    gc_chain.step(2, 1)
     gc_flat = gc[...].reshape(T, D)
     dcT[...] = dot_nt(full(2), gc_flat).astype(BF)
 
@@ -696,9 +724,10 @@
             dmp[block, :, at - block * MB : end - block * MB] = dm[j, 0:8, at - lo : end - lo]
             at = end
     dm_copies = direct(
-        3, lambda k: dmp.at[lax.rem(tp + k, TP)], lambda k: dmr.at[TP - 1 - k]
+        3, lambda k: dmp.at[lax.rem(tp + k, TP), 0:items], lambda k: dmr.at[TP - 1 - k, 0:items]
     )
-    rs2_copies = to_owners(rs2_send, rs2_recv, 2)
+    rs2_copies = to_owners(rs2_send, rs2_recv, 2, own)
+    pending.extend(rs2_copies.values())
     reduce_self.scatter_end(0)
     reduce_self.scatter_start(1)
     reduce_mlp.gather_end()
@@ -708,18 +737,18 @@
     reduce_cross.scatter_end(1)
     reduce_cross.scatter_start(2)
 
-    d_mod = dmp[tp]
+    d_mod = dmp[tp, 0:items]
     for k in range(1, TP):
         arrived(dm_copies, k)
-        d_mod = d_mod + dmr[k - 1]
+        d_mod = d_mod + dmr[k - 1, 0:items]
     low = d_mod.astype(BF)
-    lall[dp] = low.astype(F32)
-    dsil[...] = dot_nt(low, wmod[...])
-    ds_copies = direct(4, lambda k: dsil, lambda k: dsr.at[TP - 1 - k])
+    lall[dp, 0:items] = low.astype(F32)
+    dsil[0:items, :] = dot_nt(low, wmod[...])
+    ds_copies = direct(4, lambda k: dsil.at[0:items], lambda k: dsr.at[TP - 1 - k, 0:items])
 
     reduce_self.scatter_end(1)
     reduce_self.scatter_start(2)
-    dp_send(lall.at[dp], lall.at[dp], 1)
+    dp_send(lall.at[dp, 0:items], lall.at[dp, 0:items], 1)
     reduce_cross.scatter_end(2)
     reduce_cross.widen()
     reduce_cross.gather_start(2)
@@ -743,16 +772,16 @@
     reduce_cross.gather_end()
     reduce_cross.gather_start(0)
 
-    d_silu = dsil[...]
+    d_silu = dsil[0:items, :]
     for k in range(1, TP):
         arrived(ds_copies, k)
-        d_silu = d_silu + dsr[k - 1]
+        d_silu = d_silu + dsr[k - 1, 0:items]
     for item in range(items):
         value = time_ref[item]
         gate = 1.0 / (1.0 + jnp.exp(-value))
         dtime_o[item] = d_silu[item : item + 1, :] * (gate * (1.0 + value * (1.0 - gate)))
     dp_wait(eall.at[dp], eall.at[dp], 0)
-    dp_wait(lall.at[dp], lall.at[dp], 1)
+    dp_wait(lall.at[dp, 0:items], lall.at[dp, 0:items], 1)
     out_copies = [
         pltpu.make_async_copy(eall, early_o, osem.at[3, 0]),
         pltpu.make_async_copy(lall, late_o, osem.at[3, 1]),
@@ -775,64 +804,71 @@
     place, items, grads_h, early_h, late_h, dtok_h, dtime_h, dtext_h,
     dtok_o, dtime_o, dtext_o, qkv_o, attn_out_o, cross_q_o, cross_kv_o, cross_out_o, up_o, down_o, mod_o,
     gb_attn_o, gb_cross_o, gb_up_o, gb_mod_o,
-    low, full_v, kv_v, mod_v, early_v, late_v, isem, osem,
+    low, full_v, kv_v, mod_v, early_v, late_v, isem, osem, ssem,
 ):
     names = ("up", "down", "qkv", "cross_kv", "attn_out", "cross_out", "cross_q")
     outs = {
         "up": up_o, "down": down_o, "qkv": qkv_o, "attn_out": attn_out_o, "cross_out": cross_out_o,
         "cross_q": cross_q_o, "cross_kv": cross_kv_o,
     }
-    loads = {}
+    unit = 384
+    chunks = []
+    for name in names:
+        at, rows = place[name]
+        step = rows if name == "cross_kv" else math.gcd(rows, unit)
+        chunks += [(name, at + i, step, i) for i in range(0, rows, step)]
     small = [
-        pltpu.make_async_copy(early_h, early_v, isem.at[7]),
-        pltpu.make_async_copy(late_h, late_v, isem.at[8]),
+        pltpu.make_async_copy(early_h, early_v, ssem.at[0]),
+        pltpu.make_async_copy(late_h, late_v, ssem.at[1]),
     ]
     stores = [
-        pltpu.make_async_copy(dtok_h, dtok_o, osem.at[8]),
-        pltpu.make_async_copy(dtime_h, dtime_o, osem.at[9]),
-        pltpu.make_async_copy(dtext_h, dtext_o, osem.at[10]),
+        pltpu.make_async_copy(dtok_h, dtok_o, ssem.at[2]),
+        pltpu.make_async_copy(dtime_h, dtime_o, ssem.at[3]),
+        pltpu.make_async_copy(dtext_h, dtext_o, ssem.at[4]),
     ]
-    for copy in small + stores:
+    loads = [
+        pltpu.make_async_copy(grads_h.at[at : at + step], low.at[at : at + step], isem.at[i])
+        for i, (_, at, step, _) in enumerate(chunks)
+    ]
+    for copy in small + stores + loads:
         copy.start()
-    for i, name in enumerate(names):
-        at, rows = place[name]
-        loads[name] = pltpu.make_async_copy(
-            grads_h.at[at : at + rows], low.at[at : at + rows], isem.at[i]
-        )
-        loads[name].start()
-
-    def store(src, dst, i):
-        copy = pltpu.make_async_copy(src, dst, osem.at[i])
+
+    def store(src, dst, sem):
+        copy = pltpu.make_async_copy(src, dst, sem)
         copy.start()
         stores.append(copy)
 
+    for i, (name, at, step, offset) in enumerate(chunks):
+        loads[i].wait()
+        if name == "cross_kv":
+            ident = (
+                lax.broadcasted_iota(jnp.int32, (step, step), 0)
+                == lax.broadcasted_iota(jnp.int32, (step, step), 1)
+            ).astype(F32).astype(BF)
+            kv_v[...] = dot_tn(low[at : at + step, :], ident)
+            store(kv_v, outs[name], osem.at[i])
+        else:
+            full_v[at : at + step, :] = low[at : at + step, :].astype(F32)
+            store(full_v.at[at : at + step], outs[name].at[offset : offset + step], osem.at[i])
+    for copy in small:
+        copy.wait()
     dp_count, slots, D = early_v.shape
     MB = late_v.shape[2]
-    for copy in small:
-        copy.wait()
     keep = lax.rem(lax.broadcasted_iota(jnp.int32, (dp_count * slots, MB), 0), slots) < items
     late = jnp.where(keep, late_v[...].reshape(dp_count * slots, MB), 0.0)
     early = early_v[...]
-    mod_v[...] = dot_tn(early.reshape(dp_count * slots, D).astype(BF), late.astype(BF))
-    store(mod_v, mod_o, 7)
+    left, right = early.reshape(dp_count * slots, D).astype(BF), late.astype(BF)
+    parts = 3
+    rows = D // parts
+    for i in range(parts):
+        piece = slice(i * rows, (i + 1) * rows)
+        mod_v[piece, :] = dot_tn(left[:, piece], right)
+        store(mod_v.at[piece], mod_o.at[piece], ssem.at[5 + i])
     gb_mod_o[...] = jnp.sum(late, axis=0)
     sums = jnp.sum(early, axis=0)
     gb_up_o[...] = sums[3]
     gb_cross_o[...] = sums[4]
     gb_attn_o[...] = sums[5]
-    for i, name in enumerate(names):
-        at, rows = place[name]
-        loads[name].wait()
-        if name == "cross_kv":
-            ident = (
-                lax.broadcasted_iota(jnp.int32, (rows, rows), 0)
-                == lax.broadcasted_iota(jnp.int32, (rows, rows), 1)
-            ).astype(F32).astype(BF)
-            kv_v[...] = dot_tn(low[at : at + rows, :], ident)
-            store(kv_v, outs[name], i)
-        else:
-            full_v[at : at + rows, :] = low[at : at + rows, :].astype(F32)
-            store(full_v.at[at : at + rows], outs[name], i)
     for copy in stores:
         copy.wait()
 
@@ -884,7 +920,7 @@
     smem = pl.BlockSpec(memory_space=pltpu.SMEM)
     V = pltpu.VMEM
     DMA = pltpu.SemaphoreType.DMA
-    chunks = max(HL, 2)
+    chunks = max(HL, 5)
     scratch = [
         V((TP, R, D), BF), V((TP, R, D), BF), V((TP, TL, D), BF), V((TP, HW, T), BF), V((TP, R, D), BF),
         V((3 * HW, D), BF), V((D, 2 * HW), BF), V((TP, 5, HW, D), BF),
@@ -901,7 +937,7 @@
         V((6, 16, D), F32), V((TP, 8, MB), F32), V((TP - 1, 8, MB), F32), V((8, D), F32), V((TP - 1, 8, D), F32),
         V((8, D), F32), V((dp_count, 8, D), F32), V((dp_count, 8, MB), F32),
         V((total_rows, D), BF), V((room, D), BF),
-        DMA((11,)), DMA((5, TP)), DMA((5, TP)), DMA((6, 5, chunks)), DMA((6, TP, chunks)), DMA((2, 3)), DMA((2, 3)),
+        DMA((11,)), DMA((6, TP)), DMA((6, TP)), DMA((6, 5, chunks)), DMA((6, TP, chunks)), DMA((5, 3)), DMA((5, 3)),
         DMA((3, 2, 6 + extra)), DMA((3, 2, 6 + extra)), DMA((2, dp_count)), DMA((2, dp_count)), DMA((4, 2)),
     ]
     d_tokens, d_time, d_text, grads, early, late = pl.pallas_call(
@@ -939,7 +975,7 @@
         out_specs=(hbm,) * 11 + (vmem,) * 4,
         scratch_shapes=[
             V((total_rows, D), BF), V((total_rows, D), F32), V((D, 2 * HW), F32), V((D, MB), F32),
-            V((dp_count, 8, D), F32), V((dp_count, 8, MB), F32), DMA((9,)), DMA((11,)),
+            V((dp_count, 8, D), F32), V((dp_count, 8, MB), F32), DMA((16,)), DMA((16,)), DMA((8,)),
         ],
         name="finish",
         compiler_params=pltpu.CompilerParams(vmem_limit_bytes=63 * 1024 * 1024),

time: 161 us -> 153 us (0.950)
  Pallas kernels: 160 us -> 152 us
    pallas_call x1, Pallas kernels: 150 us -> 141 us  [body(): pl.pallas_call(functools.partial(layer_kernel, (dp_count, place, items)),...]
where the time goes in v2:
time: 153 us
  Pallas kernels  152 us (99%)
    pallas_call x1, Pallas kernels, body(): pl.pallas_call(functools.partial(layer_kernel, (dp_count, place, items)),...  141 us
    pallas_call x1, Pallas kernels, body(): pl.pallas_call(functools.partial(finish_kernel, place, items), out_shape=...  10.6 us

profile of v2, /device:TPU:1, one launch (start us, length us, event | category | flops | bytes accessed | tf_op | source)
XLA Modules:
  0.0 152.6 jit_solution(16529311729879081193)
XLA Ops:
  0.7 141.2 %layer.1 = (bf16[128,768]{1,0:T(8,128)(2,1)}, f32[3,1,768]{2,1,0:T(1,128)}, bf16[48,768]{1,0:T(8,128)(2,1)}, bf16[3072,768]{1,0:T(8,128)(2,1)}, f32[8,8,768]{2,1,0:T(8,128)}, /*index=5*/f32[8,8,1152]{2,1,0:T(8,128)}) custom-call(bf16[128,768]{1,0:T(8,128)(2,1)} %bitcast.13, bf16[128,768]{1,0:T(8,128)(2,1)} %bitcast.14, bf16[48,768]{1,0:T(8,128)(2,1)} %bitcast.15, ...), custom_call_target="tpu_custom_call" | custom-call | tf_op jit(solution)/shard_map/layer/pallas_call | solution.py:943
  141.9 10.6 %finish.1 = (bf16[128,768]{1,0:T(8,128)(2,1)}, f32[3,1,768]{2,1,0:T(1,128)}, bf16[48,768]{1,0:T(8,128)(2,1)}, f32[576,768]{1,0:T(8,128)}, f32[192,768]{1,0:T(8,1...) custom-call(bf16[3072,768]{1,0:T(8,128)(2,1)} %get-tuple-element.36., ...), custom_call_target="tpu_custom_call" | custom-call | tf_op jit(solution)/shard_map/finish/pallas_call | solution.py:967

commit v3 on v2

--- a/solution.py
+++ b/solution.py
@@ -226,7 +226,8 @@
     w_chain = Chain(2, lambda slot, c: wfull.at[slot, mats[c], span(places[c] * WR, WR, 16), pl.ds(wcol, WC)])
     att_chain = Chain(3, lambda slot, c: att.at[slot, c * DH : (c + 1) * DH])
     og_chain = Chain(4, lambda slot, c: og.at[slot, c * half : (c + 1) * half])
-    gc_chain = Chain(5, lambda slot, c: gc.at[slot, c * half : (c + 1) * half])
+    split = R * 5 // 8
+    gc_chain = Chain(5, lambda slot, c: gc.at[slot, c * split : R if c else split])
 
     class Plane:
         def __init__(self, index, bits):
@@ -478,7 +479,7 @@
             copies[b].start()
         return copies
 
-    halves = (slice(0, half), slice(half, R))
+    halves = (slice(0, split), slice(split, R))
     rs_first = to_owners(rs_send, rs_recv, 1, halves[0])
     early[3:4, :] = dot_nn(onehot[...], dpre[...])[items : items + 1, :]
 
@@ -652,7 +653,12 @@
             dckvT[vr, :] = dot_nt(dcT[hr, :], probs.astype(BF)).astype(BF)
         return carry
 
-    lax.fori_loop(0, HEADS // 4, cross_backward, 0)
+    cross_backward(0, 0)
+    put("cross_out", dot_nn(catT[0:HW, :], gc_flat))
+    put("cross_q", dot_nn(dcqT[0:HW, :], cross_in[...]))
+    put("cross_kv", dot_nn(dckvT[0 : 2 * HW, :], text_flat))
+    reduce_cross.scatter_start(0)
+    lax.fori_loop(1, HEADS // 4, cross_backward, 0)
     d_cross = dot_tn(dcqT[...], full(1))
     back = normalize_back(d_cross, cross_in[...].astype(F32), inv_c[...])
     grad = gc_own[...] + back[:R]
@@ -662,12 +668,10 @@
     rest = slice(R, T)
     dba[rest, :] = ((gc_flat[R:].astype(F32) + back[R:]) * gate[R:]).astype(BF)
     dOT[...] = dot_nt(wfull[0, 0], dba[...]).astype(BF)
-
-    put("cross_out", dot_nn(catT[0:HW, :], gc_flat))
-    put("cross_q", dot_nn(dcqT[0:HW, :], cross_in[...]))
-    put("cross_kv", dot_nn(dckvT[0 : 2 * HW, :], text_flat))
+    reduce_cross.scatter_end(0)
+    reduce_cross.scatter_start(1)
+
     put("attn_out", dot_nn(att[0], dba[...]))
-    reduce_cross.scatter_start(0)
     early[4:5, :] = dot_nn(onehot[...], gc_flat)[items : items + 1, :]
     early[5:6, :] = dot_nn(onehot[...], dba[...])[items : items + 1, :]
     eall[dp] = early[...]
@@ -705,11 +709,11 @@
 
     put("qkv", dot_nn(dqkvT[...], attn_in[...]))
     reduce_self.scatter_start(0)
-    reduce_cross.scatter_end(0)
-    reduce_cross.scatter_start(1)
 
     part = dot_tn(dqkvT[...], wqkvT[...])
     rs2_send[...] = part.astype(BF).reshape(TP, R, D)
+    reduce_self.scatter_end(0)
+    reduce_self.scatter_start(1)
     input_grad = rs2_send[...].reshape(T, D)
     dm[0] = dot_nn(onehot[...], input_grad)
     dm[1] = item_sums(every, input_grad.astype(F32) * na[...].astype(F32))
@@ -728,14 +732,17 @@
     )
     rs2_copies = to_owners(rs2_send, rs2_recv, 2, own)
     pending.extend(rs2_copies.values())
-    reduce_self.scatter_end(0)
-    reduce_self.scatter_start(1)
+    reduce_cross.scatter_end(1)
+    reduce_cross.scatter_start(2)
     reduce_mlp.gather_end()
     reduce_mlp.gather_start(0)
 
     dtext_o[...] = dot_tn(dckvT[:, 0:TL], wfull[:, 3:5].reshape(TP * 2 * HW, D)).astype(BF)
-    reduce_cross.scatter_end(1)
-    reduce_cross.scatter_start(2)
+    reduce_self.scatter_end(1)
+    reduce_self.scatter_start(2)
+    reduce_cross.scatter_end(2)
+    reduce_cross.widen()
+    reduce_cross.gather_start(2)
 
     d_mod = dmp[tp, 0:items]
     for k in range(1, TP):
@@ -746,32 +753,23 @@
     dsil[0:items, :] = dot_nt(low, wmod[...])
     ds_copies = direct(4, lambda k: dsil.at[0:items], lambda k: dsr.at[TP - 1 - k, 0:items])
 
-    reduce_self.scatter_end(1)
-    reduce_self.scatter_start(2)
     dp_send(lall.at[dp, 0:items], lall.at[dp, 0:items], 1)
-    reduce_cross.scatter_end(2)
-    reduce_cross.widen()
-    reduce_cross.gather_start(2)
     reduce_self.scatter_end(2)
     reduce_self.widen()
     reduce_self.gather_start(2)
-    reduce_mlp.gather_end()
     reduce_cross.gather_end()
     reduce_cross.gather_start(1)
+    reduce_mlp.gather_end()
+    dp_wait(eall.at[dp], eall.at[dp], 0)
+    out_copies = [
+        pltpu.make_async_copy(eall, early_o, osem.at[3, 0]),
+        pltpu.make_async_copy(lall, late_o, osem.at[3, 1]),
+    ]
+    out_copies[0].start()
     reduce_self.gather_end()
     reduce_self.gather_start(1)
-
-    d_in = rs2_send[0].astype(F32)
-    for k in (1, 3, 2):
-        rs2_copies[TP - k].wait_recv()
-        d_in = d_in + rs2_recv[k - 1].astype(F32)
-    normed, inverse = normalize(tok[0].astype(F32))
-    dtok_o[...] = (
-        grad_own[...] + normalize_back(d_in * (1.0 + per_frame(1, own)), normed, inverse)
-    ).astype(BF)
     reduce_cross.gather_end()
     reduce_cross.gather_start(0)
-
     d_silu = dsil[0:items, :]
     for k in range(1, TP):
         arrived(ds_copies, k)
@@ -780,16 +778,19 @@
         value = time_ref[item]
         gate = 1.0 / (1.0 + jnp.exp(-value))
         dtime_o[item] = d_silu[item : item + 1, :] * (gate * (1.0 + value * (1.0 - gate)))
-    dp_wait(eall.at[dp], eall.at[dp], 0)
     dp_wait(lall.at[dp, 0:items], lall.at[dp, 0:items], 1)
-    out_copies = [
-        pltpu.make_async_copy(eall, early_o, osem.at[3, 0]),
-        pltpu.make_async_copy(lall, late_o, osem.at[3, 1]),
-    ]
-    for copy in out_copies:
-        copy.start()
+    out_copies[1].start()
+    normed, inverse = normalize(tok[0].astype(F32))
     reduce_self.gather_end()
     reduce_self.gather_start(0)
+
+    d_in = rs2_send[0].astype(F32)
+    for k in (1, 3, 2):
+        rs2_copies[TP - k].wait_recv()
+        d_in = d_in + rs2_recv[k - 1].astype(F32)
+    dtok_o[...] = (
+        grad_own[...] + normalize_back(d_in * (1.0 + per_frame(1, own)), normed, inverse)
+    ).astype(BF)
     for chain in chains:
         chain.finish()
     reduce_cross.gather_end()
@@ -804,7 +805,7 @@
     place, items, grads_h, early_h, late_h, dtok_h, dtime_h, dtext_h,
     dtok_o, dtime_o, dtext_o, qkv_o, attn_out_o, cross_q_o, cross_kv_o, cross_out_o, up_o, down_o, mod_o,
     gb_attn_o, gb_cross_o, gb_up_o, gb_mod_o,
-    low, full_v, kv_v, mod_v, early_v, late_v, isem, osem, ssem,
+    low, full_v, kv_v, mod_v, early_v, late_v, dtok_v, dtime_v, dtext_v, isem, osem, ssem,
 ):
     names = ("up", "down", "qkv", "cross_kv", "attn_out", "cross_out", "cross_q")
     outs = {
@@ -821,16 +822,14 @@
         pltpu.make_async_copy(early_h, early_v, ssem.at[0]),
         pltpu.make_async_copy(late_h, late_v, ssem.at[1]),
     ]
-    stores = [
-        pltpu.make_async_copy(dtok_h, dtok_o, ssem.at[2]),
-        pltpu.make_async_copy(dtime_h, dtime_o, ssem.at[3]),
-        pltpu.make_async_copy(dtext_h, dtext_o, ssem.at[4]),
-    ]
+    through = [(dtok_h, dtok_v, dtok_o), (dtime_h, dtime_v, dtime_o), (dtext_h, dtext_v, dtext_o)]
+    passed = [pltpu.make_async_copy(src, mid, ssem.at[2 + i]) for i, (src, mid, _) in enumerate(through)]
+    stores = []
     loads = [
         pltpu.make_async_copy(grads_h.at[at : at + step], low.at[at : at + step], isem.at[i])
         for i, (_, at, step, _) in enumerate(chunks)
     ]
-    for copy in small + stores + loads:
+    for copy in small + passed + loads:
         copy.start()
 
     def store(src, dst, sem):
@@ -850,8 +849,10 @@
         else:
             full_v[at : at + step, :] = low[at : at + step, :].astype(F32)
             store(full_v.at[at : at + step], outs[name].at[offset : offset + step], osem.at[i])
-    for copy in small:
+    for copy in small + passed:
         copy.wait()
+    for i, (_, mid, dst) in enumerate(through):
+        store(mid, dst, ssem.at[8 + i])
     dp_count, slots, D = early_v.shape
     MB = late_v.shape[2]
     keep = lax.rem(lax.broadcasted_iota(jnp.int32, (dp_count * slots, MB), 0), slots) < items
@@ -975,7 +976,8 @@
         out_specs=(hbm,) * 11 + (vmem,) * 4,
         scratch_shapes=[
             V((total_rows, D), BF), V((total_rows, D), F32), V((D, 2 * HW), F32), V((D, MB), F32),
-            V((dp_count, 8, D), F32), V((dp_count, 8, MB), F32), DMA((16,)), DMA((16,)), DMA((8,)),
+            V((dp_count, 8, D), F32), V((dp_count, 8, MB), F32), V((R, D), BF), V((items, 1, D), F32), V((TL, D), BF),
+            DMA((16,)), DMA((16,)), DMA((11,)),
         ],
         name="finish",
         compiler_params=pltpu.CompilerParams(vmem_limit_bytes=63 * 1024 * 1024),

time: 153 us -> 148 us (0.967)
  Pallas kernels: 152 us -> 146 us
    pallas_call x1, Pallas kernels: 10.6 us -> 6.92 us  [body(): pl.pallas_call(functools.partial(finish_kernel, place, items), out_shape=...]
    pallas_call x1, Pallas kernels: 141 us -> 139 us  [body(): pl.pallas_call(functools.partial(layer_kernel, (dp_count, place, items)),...]
where the time goes in v3:
time: 148 us; the launch traced here: 147 us
  Pallas kernels  146 us (99%)
    pallas_call x1, Pallas kernels, body(): pl.pallas_call(functools.partial(layer_kernel, (dp_count, place, items)),...  139 us
    pallas_call x1, Pallas kernels, body(): pl.pallas_call(functools.partial(finish_kernel, place, items), out_shape=...  6.92 us

profile of v3, /device:TPU:1, one launch (start us, length us, event | category | flops | bytes accessed | tf_op | source)
XLA Modules:
  0.0 147.1 jit_solution(1711911049745222643)
XLA Ops:
  0.7 139.4 %layer.1 = (bf16[128,768]{1,0:T(8,128)(2,1)}, f32[3,1,768]{2,1,0:T(1,128)}, bf16[48,768]{1,0:T(8,128)(2,1)}, bf16[3072,768]{1,0:T(8,128)(2,1)}, f32[8,8,768]{2,1,0:T(8,128)}, /*index=5*/f32[8,8,1152]{2,1,0:T(8,128)}) custom-call(bf16[128,768]{1,0:T(8,128)(2,1)} %bitcast.13, bf16[128,768]{1,0:T(8,128)(2,1)} %bitcast.14, bf16[48,768]{1,0:T(8,128)(2,1)} %bitcast.15, ...), custom_call_target="tpu_custom_call" | custom-call | tf_op jit(solution)/shard_map/layer/pallas_call | solution.py:944
  140.0 6.9 %finish.1 = (bf16[128,768]{1,0:T(8,128)(2,1)}, f32[3,1,768]{2,1,0:T(1,128)}, bf16[48,768]{1,0:T(8,128)(2,1)}, f32[576,768]{1,0:T(8,128)}, f32[192,768]{1,0:T(8,1...) custom-call(bf16[3072,768]{1,0:T(8,128)(2,1)} %get-tuple-element.36., ...), custom_call_target="tpu_custom_call" | custom-call | tf_op jit(solution)/shard_map/finish/pallas_call | solution.py:968

commit v4 on v3

--- a/solution.py
+++ b/solution.py
@@ -449,7 +449,8 @@
             catT[span(h * DH, DH, DH), :] = dot_nn(vT, probs.astype(BF)).astype(BF)
         return carry
 
-    lax.fori_loop(0, HEADS // 4, cross_forward, 0)
+    for g in range(HEADS // 4):
+        cross_forward(g, 0)
     og_chain.step(2, 0)
     og_chain.step(2, 1)
     normed, inverse = normalize(stream_a[...] + dot_tn(catT[...], full(2)) + b_cross_out)
@@ -697,6 +698,9 @@
 
     dp_send(eall.at[dp], eall.at[dp], 0)
 
+    reduce_mlp.gather_end()
+    reduce_mlp.gather_start(0)
+
     for h in range(HL):
         q0 = h * 3 * DH
         hr = slice(h * DH, (h + 1) * DH)
@@ -734,8 +738,6 @@
     pending.extend(rs2_copies.values())
     reduce_cross.scatter_end(1)
     reduce_cross.scatter_start(2)
-    reduce_mlp.gather_end()
-    reduce_mlp.gather_start(0)
 
     dtext_o[...] = dot_tn(dckvT[:, 0:TL], wfull[:, 3:5].reshape(TP * 2 * HW, D)).astype(BF)
     reduce_self.scatter_end(1)
@@ -770,6 +772,19 @@
     reduce_self.gather_start(1)
     reduce_cross.gather_end()
     reduce_cross.gather_start(0)
+    dp_wait(lall.at[dp, 0:items], lall.at[dp, 0:items], 1)
+    out_copies[1].start()
+    normed, inverse = normalize(tok[0].astype(F32))
+    reduce_self.gather_end()
+    reduce_self.gather_start(0)
+
+    d_in = rs2_send[0].astype(F32)
+    for k in (1, 3, 2):
+        rs2_copies[TP - k].wait_recv()
+        d_in = d_in + rs2_recv[k - 1].astype(F32)
+    dtok_o[...] = (
+        grad_own[...] + normalize_back(d_in * (1.0 + per_frame(1, own)), normed, inverse)
+    ).astype(BF)
     d_silu = dsil[0:items, :]
     for k in range(1, TP):
         arrived(ds_copies, k)
@@ -778,19 +793,6 @@
         value = time_ref[item]
         gate = 1.0 / (1.0 + jnp.exp(-value))
         dtime_o[item] = d_silu[item : item + 1, :] * (gate * (1.0 + value * (1.0 - gate)))
-    dp_wait(lall.at[dp, 0:items], lall.at[dp, 0:items], 1)
-    out_copies[1].start()
-    normed, inverse = normalize(tok[0].astype(F32))
-    reduce_self.gather_end()
-    reduce_self.gather_start(0)
-
-    d_in = rs2_send[0].astype(F32)
-    for k in (1, 3, 2):
-        rs2_copies[TP - k].wait_recv()
-        d_in = d_in + rs2_recv[k - 1].astype(F32)
-    dtok_o[...] = (
-        grad_own[...] + normalize_back(d_in * (1.0 + per_frame(1, own)), normed, inverse)
-    ).astype(BF)
     for chain in chains:
         chain.finish()
     reduce_cross.gather_end()

time: 148 us -> 148 us (level)
  no operation moved by 1% of the time
where the time goes in v4:
time: 148 us; the launch traced here: 147 us
  Pallas kernels  147 us (99%)
    pallas_call x1, Pallas kernels, body(): pl.pallas_call(functools.partial(layer_kernel, (dp_count, place, items)),...  140 us
    pallas_call x1, Pallas kernels, body(): pl.pallas_call(functools.partial(finish_kernel, place, items), out_shape=...  6.92 us

profile of v4, /device:TPU:1, one launch (start us, length us, event | category | flops | bytes accessed | tf_op | source)
XLA Modules:
  0.0 147.5 jit_solution(6074773588715554364)
XLA Ops:
  0.7 139.7 %layer.1 = (bf16[128,768]{1,0:T(8,128)(2,1)}, f32[3,1,768]{2,1,0:T(1,128)}, bf16[48,768]{1,0:T(8,128)(2,1)}, bf16[3072,768]{1,0:T(8,128)(2,1)}, f32[8,8,768]{2,1,0:T(8,128)}, /*index=5*/f32[8,8,1152]{2,1,0:T(8,128)}) custom-call(bf16[128,768]{1,0:T(8,128)(2,1)} %bitcast.13, bf16[128,768]{1,0:T(8,128)(2,1)} %bitcast.14, bf16[48,768]{1,0:T(8,128)(2,1)} %bitcast.15, ...), custom_call_target="tpu_custom_call" | custom-call | tf_op jit(solution)/shard_map/layer/pallas_call | solution.py:946
  140.4 6.9 %finish.1 = (bf16[128,768]{1,0:T(8,128)(2,1)}, f32[3,1,768]{2,1,0:T(1,128)}, bf16[48,768]{1,0:T(8,128)(2,1)}, f32[576,768]{1,0:T(8,128)}, f32[192,768]{1,0:T(8,1...) custom-call(bf16[3072,768]{1,0:T(8,128)(2,1)} %get-tuple-element.36., ...), custom_call_target="tpu_custom_call" | custom-call | tf_op jit(solution)/shard_map/finish/pallas_call | solution.py:970
